TPU v7x, 256 devices: a whole 4x4x8 slice. The times are simulated.
256 devices in a mesh: dom: 32 (over y, z), feat: 8 (over x, core).
Axes of the slice: x: 4, y: 4, z: 8, core: 2. Of those that a mesh axis runs over, the one named last changes fastest.
Arguments:
- feats: bfloat16 [131072, 1024], P('dom', 'feat'), may hold values from -6 to 6
- projection: bfloat16 [1024, 512], P('feat'), may hold values from -0.1875 to 0.1875
- tiles: bfloat16 [8192, 4, 128, 128], P(('dom', 'feat')), may hold values from -0.25 to 0.25
- slot_owner: int32 [8192, 1], P(('dom', 'feat')), may hold values from 0 to 31; in each aligned block of 32 rows (0 to 31, 32 to 63, ...) at most 2 rows name the same one
- slot_block: int32 [8192, 1], P(('dom', 'feat')), may hold values from 0 to 3
- source_block: int32 [8192, 4], P(('dom', 'feat')), may hold values from 0 to 3
- counts: int32 [131072], P(('dom', 'feat')), may hold values from 1 to 4
- out_grad: bfloat16 [131072, 256], P(('dom', 'feat')), may hold values from -0.015625 to 0.015625
Outputs:
- activated: bfloat16 [131072, 256], P(('dom', 'feat'))
- weight_grad: float32 [1024, 512], P('feat')
Inputs may be any that keep to these rules, and one draw needn't show every extreme that they name: `slot_owner`: among the 32 sent rows of one device, no dom index is named more than 2 times; some device names one exactly 2 times.
All inputs are finite; a program needn't handle non-finite values.
Results may differ from a plain program's by a relative error of at most 0.0059.
Values may be sent and summed in bfloat16 or wider, within the bound.
A program may use at most 128 MiB of HBM per device.

v0:
```python
import jax
import jax.numpy as jnp
from jax import lax
from jax.sharding import PartitionSpec as P


def local(feats, projection, tiles, slot_owner, slot_block, source_block, counts, out_grad):
    tile_size = tiles.shape[-1]
    slot_count = tiles.shape[0]
    per_slot = tiles.shape[1]
    out_width = out_grad.shape[1]
    node_rows = out_grad.shape[0]
    block_count = node_rows // tile_size
    dom_count = lax.axis_size("dom")
    capacity = max(2, 2 * slot_count // dom_count)
    flat_width = tile_size * out_width
    projected = lax.psum_scatter(
        jnp.dot(feats, projection, preferred_element_type=jnp.float32),
        "feat",
        scatter_dimension=0,
        tiled=True,
    ).astype(jnp.bfloat16)
    neighbour = projected[:, :out_width].reshape(block_count, tile_size, out_width)
    self_part = projected[:, out_width:]
    picked = neighbour[source_block]
    contribution = jnp.einsum("skij,skjh->sih", tiles, picked, preferred_element_type=jnp.float32)
    contribution = contribution.astype(jnp.bfloat16).reshape(slot_count, flat_width)
    slot_dest = slot_owner[:, 0]
    dest_block = slot_block[:, 0]
    dest_hot = (slot_dest[:, None] == jnp.arange(dom_count, dtype=jnp.int32)[None, :]).astype(
        jnp.int32
    )
    before = jnp.cumsum(dest_hot, axis=0) - dest_hot
    position = jnp.sum(before * dest_hot, axis=1)
    slot_index = slot_dest * capacity + position
    placing = jnp.arange(dom_count * capacity, dtype=jnp.int32)[:, None] == slot_index[None, :]
    outgoing = jnp.dot(
        placing.astype(jnp.bfloat16), contribution, preferred_element_type=jnp.float32
    )
    outgoing = outgoing.astype(jnp.bfloat16).reshape(dom_count, capacity, flat_width)
    labels = jnp.sum(placing.astype(jnp.int32) * (dest_block + 1)[None, :], axis=1) - 1
    labels = labels.reshape(dom_count, capacity)
    incoming, got_labels = (
        lax.all_to_all(outgoing, "dom", split_axis=0, concat_axis=0, tiled=True),
        lax.all_to_all(labels, "dom", split_axis=0, concat_axis=0, tiled=True),
    )
    incoming = incoming.reshape(dom_count * capacity, flat_width)
    receive_hot = (
        jnp.arange(block_count, dtype=jnp.int32)[:, None] == got_labels.reshape(-1)[None, :]
    ).astype(jnp.bfloat16)
    summed = jnp.dot(receive_hot, incoming, preferred_element_type=jnp.float32).reshape(
        node_rows, out_width
    )
    degree = counts.astype(jnp.float32)[:, None]
    preact = summed / degree + self_part.astype(jnp.float32)
    sigma = jax.nn.sigmoid(preact)
    activated = (preact * sigma).astype(jnp.bfloat16)
    grad_pre = out_grad.astype(jnp.float32) * sigma * (1.0 + preact * (1.0 - sigma))
    grad_self = grad_pre.astype(jnp.bfloat16)
    grad_sum = (grad_pre / degree).astype(jnp.bfloat16).reshape(block_count, flat_width)
    sending_back = jnp.dot(receive_hot.T, grad_sum, preferred_element_type=jnp.float32)
    sending_back = sending_back.astype(jnp.bfloat16).reshape(dom_count, capacity, flat_width)
    returned = lax.all_to_all(sending_back, "dom", split_axis=0, concat_axis=0, tiled=True).reshape(
        dom_count * capacity, flat_width
    )
    slot_grad = jnp.dot(
        placing.T.astype(jnp.bfloat16), returned, preferred_element_type=jnp.float32
    )
    slot_grad = slot_grad.astype(jnp.bfloat16).reshape(slot_count, tile_size, out_width)
    products = jnp.einsum("skij,sih->skjh", tiles, slot_grad, preferred_element_type=jnp.float32)
    source_hot = (
        jnp.arange(block_count, dtype=jnp.int32)[:, None] == source_block.reshape(-1)[None, :]
    ).astype(jnp.float32)
    flat_products = products.reshape(slot_count * per_slot, tile_size, out_width)
    grad_neigh = jnp.einsum(
        "bn,njh->bjh", source_hot, flat_products, precision=lax.Precision.HIGHEST
    )
    grad_neigh = grad_neigh.astype(jnp.bfloat16).reshape(node_rows, out_width)
    grad_proj = jnp.concatenate([grad_neigh, grad_self], axis=1)
    partial_grad = lax.dot_general(
        feats,
        lax.all_gather(grad_proj, "feat", axis=0, tiled=True),
        (((0,), (0,)), ((), ())),
        preferred_element_type=jnp.float32,
    )
    weight_grad = lax.psum(partial_grad, "dom")
    return (activated, weight_grad)


def solution(mesh):
    placed = (
        P("dom", "feat"),
        P("feat", None),
        P(("dom", "feat"), None, None, None),
        P(("dom", "feat"), None),
        P(("dom", "feat"), None),
        P(("dom", "feat"), None),
        P(("dom", "feat")),
        P(("dom", "feat"), None),
    )
    return jax.shard_map(
        local,
        mesh=mesh,
        in_specs=placed,
        out_specs=(P(("dom", "feat"), None), P("feat", None)),
        check_vma=False,
    )
```

profile of v0, /device:TPU:1, one launch (start us, length us, event | category | flops | bytes accessed | tf_op | source)
XLA Modules:
  0.0 566.8 jit_solution(17779581834681642743)
XLA Ops:
  7.2 0.0 copy-start
  7.2 0.0 reduce-scatter.2.cloned.1.call-start
  7.2 1.2 copy-done
  8.4 5.4 fusion.12
  13.8 0.0 copy-start.6
  13.8 0.0 copy-start.8
  13.8 0.0 copy-start.5
  13.8 0.0 reduce-scatter.2.cloned.1.call-update
  13.8 0.6 copy-done.6
  14.4 0.1 fusion.3
  14.5 0.1 reduce_window_sum.11
  14.6 0.2 select_reduce_fusion.1
  14.7 0.0 copy-done.8
  14.8 0.1 select_reduce_fusion
  14.9 0.7 sub.14
  15.6 12.0 %all-to-all-start = ((s32[32,1,2]{2,1,0:T(1,128)}), s32[32,1,2]{2,1,0:T(1,128)S(1)}, u32[]{:S(2)}, u32[]{:S(2)}) async-start(s32[32,1,2]{2,1,0:T(1,128)} %bitcast.2), calls=%async_computation | async-start | bytes 32768 | tf_op jit(solution)/shard_map/all_to_all | solution.py:45
  27.6 0.0 copy-done.5
  27.7 0.1 copy.35
  27.7 0.1 reshape.85
  27.9 44.3 %reduce-scatter.2.cloned.1.call-done = f32[512,512]{1,0:T(8,128)} async-done(((f32[4096,512]{1,0:T(8,128)}), f32[512,512]{1,0:T(8,128)}) %reduce-scatter.2.cloned.1.call-update) | async-done | bytes 1048592 | tf_op jit(solution)/shard_map/reduce_scatter | solution.py:17
  72.2 1.3 convert_element_type.48
  73.5 0.0 copy-start.2
  73.5 0.8 copy-done.2
  74.3 6.5 %gather_fusion = bf16[128,128,256]{2,1,0:T(8,128)(2,1)} fusion(bf16[4,128,256]{2,1,0:T(8,128)(2,1)S(1)} %bitcast.46, s32[1024]{0:T(1024)S(1)} %pad_clamp_fusion), kind=kCustom, calls=%fused_computation | custom fusion | bytes 16777728 | tf_op jit(solution)/shard_map/gather | solution.py:25
  80.8 7.0 %fusion.2 = bf16[32,128,256]{1,2,0:T(8,128)(2,1)S(1)} fusion(bf16[32,4,128,256]{3,2,1,0:T(8,128)(2,1)} %bitcast.48, bf16[32,4,128,128]{3,2,1,0:T(8,128)(2,1)} %param.10), kind=kOutput, calls=%fused_computation.7 | convolution fusion | flops 1074790400 | bytes 14680064 | tf_op jit(solution)/shard_map/skij,skjh->sih/dot_general | solution.py:26
  87.8 2.9 copy.47
  90.7 4.9 convolution_convert_fusion.1
  95.6 7.6 %reshape.74 = bf16[32,2,32768]{2,1,0:T(2,128)(2,1)} reshape(bf16[64,32768]{1,0:T(8,128)(2,1)} %convolution_convert_fusion.1) | data formatting | bytes 8388608 | tf_op jit(solution)/shard_map/reshape | solution.py:40
  103.3 0.0 all-to-all-done
  103.3 10.0 %all-to-all-start.1 = ((bf16[32,2,32768]{2,1,0:T(2,128)(2,1)}), bf16[32,2,32768]{2,1,0:T(2,128)(2,1)}, u32[]{:S(2)}, u32[]{:S(2)}) async-start(bf16[32,2,32768]{2,1,0:T(2,128)(2,1)} %reshape.74), calls=%async_computation.2 | async-start | bytes 8388608 | tf_op jit(solution)/shard_map/all_to_all | solution.py:44
  113.3 0.0 copy-done.7
  113.3 0.5 broadcast.49
  113.9 0.7 reduce.3
  114.6 0.1 eq.63
  114.7 91.6 %all-to-all-done.1 = bf16[32,2,32768]{2,1,0:T(2,128)(2,1)} async-done(((bf16[32,2,32768]{2,1,0:T(2,128)(2,1)}), bf16[32,2,32768]{2,1,0:T(2,128)(2,1)}, u32[]{:S(2)}, u32[]{:S(2)}) %all-to-all-start.1) | async-done | bytes 4194336 | tf_op jit(solution)/shard_map/all_to_all | solution.py:44
  206.3 7.3 %reshape.75 = bf16[64,32768]{1,0:T(8,128)(2,1)} reshape(bf16[32,2,32768]{2,1,0:T(2,128)(2,1)} %all-to-all-done.1) | data formatting | bytes 8388608 | tf_op jit(solution)/shard_map/reshape | solution.py:47
  213.6 2.9 fusion.6
  216.5 0.4 reshape.76
  216.8 0.0 copy-done.3
  216.8 0.0 copy-done.4
  216.9 1.1 divide_convert_fusion
  218.0 0.2 reshape.77
  218.1 3.2 convolution_convert_fusion
  221.4 7.6 %reshape.78 = bf16[32,2,32768]{2,1,0:T(2,128)(2,1)} reshape(bf16[64,32768]{1,0:T(8,128)(2,1)} %convolution_convert_fusion) | data formatting | bytes 8388608 | tf_op jit(solution)/shard_map/reshape | solution.py:62
  229.0 9.1 %all-to-all-start.2 = ((bf16[32,2,32768]{2,1,0:T(2,128)(2,1)}), bf16[32,2,32768]{2,1,0:T(2,128)(2,1)}, u32[]{:S(2)}, u32[]{:S(2)}) async-start(bf16[32,2,32768]{2,1,0:T(2,128)(2,1)} %reshape.78), calls=%async_computation.3 | async-start | bytes 8388608 | tf_op jit(solution)/shard_map/all_to_all | solution.py:63
  238.1 0.0 all-gather.2.cloned.1.call-start
  238.2 0.1 copy.38
  238.3 0.1 eq.67
  238.4 93.5 %all-to-all-done.2 = bf16[32,2,32768]{2,1,0:T(2,128)(2,1)} async-done(((bf16[32,2,32768]{2,1,0:T(2,128)(2,1)}), bf16[32,2,32768]{2,1,0:T(2,128)(2,1)}, u32[]{:S(2)}, u32[]{:S(2)}) %all-to-all-start.2) | async-done | bytes 4194336 | tf_op jit(solution)/shard_map/all_to_all | solution.py:63
  331.8 7.3 %reshape.79 = bf16[64,32768]{1,0:T(8,128)(2,1)} reshape(bf16[32,2,32768]{2,1,0:T(2,128)(2,1)} %all-to-all-done.2) | data formatting | bytes 8388608 | tf_op jit(solution)/shard_map/reshape | solution.py:63
  339.1 3.1 convolution_convert_fusion.2
  342.2 0.5 copy.48
  342.7 0.0 copy-done.1
  342.7 8.1 %fusion = f32[32,256,4,128]{3,1,2,0:T(8,128)} fusion(bf16[32,4,128,128]{3,2,1,0:T(8,128)(2,1)S(1)} %copy-done.1, bf16[32,128,256]{2,1,0:T(8,128)(2,1)S(1)} %bitcast.52), kind=kOutput, calls=%fused_computation.5 | convolution fusion | flops 1073741824 | bytes 23068672 | tf_op jit(solution)/shard_map/skij,sih->skjh/dot_general | solution.py:70
  350.8 17.7 %copy.40 = f32[128,128,256]{2,0,1:T(8,128)} copy(f32[128,128,256]{1,2,0:T(8,128)} %bitcast.47) | data formatting | bytes 33554432 | tf_op jit(solution)/shard_map/reshape | solution.py:74
  368.5 9.0 %convolution_convert_fusion.3 = bf16[4,128,256]{2,0,1:T(4,128)(2,1)S(1)} fusion(f32[128,128,256]{2,0,1:T(8,128)} %copy.40, s32[128]{0:T(128)S(1)} %eq.67), kind=kOutput, calls=%fused_computation.8 | convolution fusion | flops 201458176 | bytes 17039872 | tf_op jit(solution)/shard_map/bn,njh->bjh/dot_general | solution.py:75
  377.5 0.8 pad_maximum_fusion
  378.4 0.0 all-gather.2.cloned.1.call-update
  378.4 0.0 all-reduce.2.cloned.1.call-start
  378.4 36.3 %all-gather.2.cloned.1.call-done = bf16[4096,512]{1,0:T(8,128)(2,1)} async-done(((bf16[512,512]{1,0:T(8,128)(2,1)}), bf16[4096,512]{1,0:T(8,128)(2,1)}) %all-gather.2.cloned.1.call-update) | async-done | bytes 4194320 | tf_op jit(solution)/shard_map/all_gather | solution.py:82
  414.8 4.2 convolution_bitcast_fusion
  418.9 0.0 all-reduce.2.cloned.1.call-update
  419.0 139.5 %all-reduce.2.cloned.1.call-done = f32[128,512]{0,1:T(8,128)} async-done(((f32[128,512]{0,1:T(8,128)}), f32[128,512]{0,1:T(8,128)}) %all-reduce.2.cloned.1.call-update) | async-done | bytes 262160 | tf_op jit(solution)/shard_map/psum | solution.py:86
  558.5 1.8 copy.42
  (12 shorter events, 0.1 us)
Async XLA Ops:
  7.2 1.2 copy-start
  7.2 65.0 %reduce-scatter.2.cloned.1.call-start = ((), (), s32[]{:S(2)}) async-start(), calls=%async_computation.4 | async-start | bytes 9437184 | tf_op jit(solution)/shard_map/reduce_scatter | solution.py:17
  13.8 0.7 copy-start.6
  13.8 1.0 copy-start.8
  13.8 13.9 %copy-start.5 = (s32[32,4]{0,1:T(4,128)S(1)}, s32[32,4]{0,1:T(4,128)}, u32[]{:S(2)}) copy-start(s32[32,4]{0,1:T(4,128)} %param.13) | copy-start | bytes 1540
  15.6 87.7 %all-to-all-start = ((s32[32,1,2]{2,1,0:T(1,128)}), s32[32,1,2]{2,1,0:T(1,128)S(1)}, u32[]{:S(2)}, u32[]{:S(2)}) async-start(s32[32,1,2]{2,1,0:T(1,128)} %bitcast.2), calls=%async_computation | async-start | bytes 32768 | tf_op jit(solution)/shard_map/all_to_all | solution.py:45
  73.5 0.8 copy-start.2
  103.3 10.0 %copy-start.7 = (s32[512]{0:T(512)S(1)}, s32[512]{0:T(512)}, u32[]{:S(2)}) copy-start(s32[512]{0:T(512)} %param.14) | copy-start | bytes 6148
  103.3 103.0 %all-to-all-start.1 = ((bf16[32,2,32768]{2,1,0:T(2,128)(2,1)}), bf16[32,2,32768]{2,1,0:T(2,128)(2,1)}, u32[]{:S(2)}, u32[]{:S(2)}) async-start(bf16[32,2,32768]{2,1,0:T(2,128)(2,1)} %reshape.74), calls=%async_computation.2 | async-start | bytes 8388608 | tf_op jit(solution)/shard_map/all_to_all | solution.py:44
  213.6 3.3 copy-start.3
  213.6 3.3 copy-start.4
  229.0 102.8 %all-to-all-start.2 = ((bf16[32,2,32768]{2,1,0:T(2,128)(2,1)}), bf16[32,2,32768]{2,1,0:T(2,128)(2,1)}, u32[]{:S(2)}, u32[]{:S(2)}) async-start(bf16[32,2,32768]{2,1,0:T(2,128)(2,1)} %reshape.78), calls=%async_computation.3 | async-start | bytes 8388608 | tf_op jit(solution)/shard_map/all_to_all | solution.py:63
  238.1 176.6 %all-gather.2.cloned.1.call-start = ((), (), s32[]{:S(2)}) async-start(), calls=%async_computation.5 | async-start | bytes 4718592 | tf_op jit(solution)/shard_map/all_gather | solution.py:82
  339.1 3.6 copy-start.1
  378.4 180.1 %all-reduce.2.cloned.1.call-start = ((), (), s32[]{:S(2)}) async-start(), calls=%async_computation.6 | async-start | bytes 524288 | tf_op jit(solution)/shard_map/psum | solution.py:86
Sparse Core Ops, SparseCore 0:
  13.9 58.2 reduce-scatter.1
  378.5 36.2 all-gather.1
  419.1 139.3 all-reduce.1
where the time goes:
time: 572 us; the launch traced here: 567 us
  waiting for transfers between devices  405 us (71%)
  local copies, waits for them, and re-layouts  64.1 us (11%)
  matrix products  47.8 us (8%)
  starting transfers between devices  31.3 us (5%)
  between operations  13.9 us (2%)
    psum x1, waiting for transfers between devices, local(): weight_grad = lax.psum(partial_grad, 'dom')  139 us
    all_to_all x1, waiting for transfers between devices, local(): lax.all_to_all(sending_back, 'dom', split_axis=0, concat_axis=0, tiled=True)  93.5 us
    all_to_all x1, waiting for transfers between devices, local(): lax.all_to_all(outgoing, 'dom', split_axis=0, concat_axis=0, tiled=True)  91.6 us
    reduce_scatter x1, waiting for transfers between devices, local(): lax.psum_scatter(jnp.dot(feats, projection, preferred_element_type=jnp.fl...  44.3 us
    all_gather x1, waiting for transfers between devices, local(): lax.all_gather(grad_proj, 'feat', axis=0, tiled=True)  36.3 us
    reshape x1, local copies, waits for them, and re-layouts, local(): products.reshape(slot_count * per_slot, tile_size, out_width)  17.7 us
    all_to_all x1, starting transfers between devices, local(): lax.all_to_all(labels, 'dom', split_axis=0, concat_axis=0, tiled=True)  12 us
  transfers between devices with their start and end apart: 6, of which 5 were waited for; matrix products, arithmetic and copies ran while one was open for 6% of the time, Pallas kernels for 0%

commit v1 on v0

v1 whole, which is shorter than its diff:
```python
import jax
import jax.numpy as jnp
from jax import lax
from jax.experimental import pallas as pl
from jax.experimental.pallas import tpu as pltpu
from jax.sharding import PartitionSpec as P

MESH = pl.DeviceIdType.MESH
NY, NZ, NX, NC = 4, 8, 4, 2
NF = NX * NC
BLK = 128
NB = 4
HID = 256
ROWS = NB * BLK
KB = 4
SLOTS = 32
CAP = 2
BF, F32 = jnp.bfloat16, jnp.float32


def table_kernel(owner_ref, block_ref, source_ref, idx_ref, lab_ref, src_ref, count_ref):
    def clear(p, carry):
        idx_ref[p] = 0
        lab_ref[p] = -1
        for k in range(KB):
            src_ref[p * KB + k] = 0
        return carry

    lax.fori_loop(0, NY * NZ * CAP, clear, 0)

    def clear_count(o, carry):
        count_ref[o] = 0
        return carry

    lax.fori_loop(0, NY * NZ, clear_count, 0)

    def place(s, carry):
        owner = owner_ref[s]
        seen = count_ref[owner]
        count_ref[owner] = seen + 1
        p = owner * CAP + seen
        idx_ref[p] = s
        lab_ref[p] = block_ref[s]
        for k in range(KB):
            src_ref[p * KB + k] = source_ref[s * KB + k]
        return carry

    lax.fori_loop(0, SLOTS, place, 0)


def main_kernel(
    idx, lab, src, feats, proj, tiles, out_grad, inv_deg,
    act_out, wg_out,
    fb, pb, tb, ogb, nb, selfb, ftb, ttb,
    ls, lr, cs, yr, ms, zr, sm,
    ga, bs, br, gs, gacc, prod,
    pw, rc, x1, rx, y1, ry, z1, rz, zt, zg, yt, yg,
    loc_sem, f_s, f_r, pn_s, pn_r, ps_s, ps_r, l_s, l_r,
    yf_s, yf_r, zf_s, zf_r, ag_s, ag_r, yb_s, yb_r,
    rc_s, rc_r, rx_s, rx_r, ry_s, ry_r, rz_s, rz_r, zg_s, zg_r, yg_s, yg_r,
):
    d = lax.axis_index("dom")
    f = lax.axis_index("feat")
    y, z = d // NZ, d % NZ
    x, c = f // NC, f % NC

    def to_feat(g):
        return (d, g)

    def to_yz(yy, zz):
        return (yy * NZ + zz, f)

    def remote(a, b, s, r, dev):
        return pltpu.make_async_remote_copy(
            src_ref=a, dst_ref=b, send_sem=s, recv_sem=r, device_id=dev, device_id_type=MESH
        )

    own_f = pltpu.make_async_copy(feats.at[f], fb.at[f], loc_sem.at[0])
    own_p = pltpu.make_async_copy(proj, pb.at[f], loc_sem.at[1])
    own_t = pltpu.make_async_copy(tiles, tb, loc_sem.at[2])
    own_g = pltpu.make_async_copy(out_grad, ogb, loc_sem.at[3])
    own_f.start()
    own_p.start()

    barrier = pltpu.get_barrier_semaphore()
    for o in range(1, NF):
        pl.semaphore_signal(barrier, inc=1, device_id=to_feat((f + o) % NF), device_id_type=MESH)
    for o in range(1, NY):
        pl.semaphore_signal(barrier, inc=1, device_id=to_yz((y + o) % NY, z), device_id_type=MESH)
    for o in range(1, NZ):
        pl.semaphore_signal(barrier, inc=1, device_id=to_yz(y, (z + o) % NZ), device_id_type=MESH)
    pl.semaphore_wait(barrier, NF + NY + NZ - 3)

    def f_copy(o):
        g = (f + o) % NF
        return remote(feats.at[g], fb.at[f], f_s.at[o], f_r.at[NF - o], to_feat(g))

    def p_copy(o, half, s, r):
        g = (f + o) % NF
        cols = pl.ds(half * HID, HID)
        return remote(proj.at[:, cols], pb.at[f, :, cols], s.at[o], r.at[NF - o], to_feat(g))

    for o in range(1, NF):
        f_copy(o).start()
        p_copy(o, 0, pn_s, pn_r).start()
    own_t.start()
    own_g.start()
    for o in range(1, NF):
        p_copy(o, 1, ps_s, ps_r).start()

    for o in range(NY):
        yy = (y + o) % NY

        def label_row(j, carry):
            ls[o, pl.ds(j, 1), :] = jnp.full((1, HID), lab[yy * (NZ * CAP) + j], jnp.int32)
            return carry

        lax.fori_loop(0, NZ * CAP, label_row, 0)

    def l_copy(o):
        return remote(ls.at[o], lr.at[NY - o], l_s.at[o], l_r.at[NY - o], to_yz((y + o) % NY, z))

    for o in range(1, NY):
        l_copy(o).start()
    lr[0] = ls[0]

    own_f.wait()
    own_p.wait()
    sm[...] = jnp.dot(fb[f], pb[f, :, :HID], preferred_element_type=F32)
    for o in range(1, NF):
        g = (f + o) % NF
        pltpu.make_async_copy(fb.at[g], fb.at[g], f_r.at[o]).wait()
        half = pb.at[g, :, pl.ds(0, HID)]
        pltpu.make_async_copy(half, half, pn_r.at[o]).wait()
        sm[...] += jnp.dot(fb[g], pb[g, :, :HID], preferred_element_type=F32)
    nb[...] = sm[...].astype(BF).reshape(NB, BLK, HID)
    own_t.wait()

    def far_first(t):
        return (z + NZ // 2 + (1 - 2 * (t % 2)) * ((t + 1) // 2)) % NZ

    def near_first(q):
        return (z + NZ + (1 - 2 * (q % 2)) * ((q + 1) // 2)) % NZ

    def yf_copy(t, o):
        return remote(
            cs.at[t, o], yr.at[t, NY - o], yf_s.at[t, o], yf_r.at[t, NY - o], to_yz((y + o) % NY, z)
        )

    def contribute(t, carry):
        zz = far_first(t)
        for o in range(1, NY + 1):
            r = o % NY
            yy = (y + r) % NY
            for i in range(CAP):
                p = (yy * NZ + zz) * CAP + i
                s = idx[p]
                total = None
                for k in range(0, KB, 2):
                    left = jnp.concatenate([tb[s, k], tb[s, k + 1]], axis=1)
                    right = jnp.concatenate(
                        [nb[src[p * KB + k]], nb[src[p * KB + k + 1]]], axis=0
                    )
                    part = jnp.dot(left, right, preferred_element_type=F32)
                    total = part if total is None else total + part
                if r:
                    cs[t, r, i] = total.astype(BF)
                else:
                    yr[t, 0, i] = total.astype(BF)
            if r:
                yf_copy(t, r).start()
        return carry

    lax.fori_loop(0, NZ, contribute, 0)

    sm[...] = jnp.dot(fb[f], pb[f, :, HID:], preferred_element_type=F32)
    for o in range(1, NF):
        g = (f + o) % NF
        half = pb.at[g, :, pl.ds(HID, HID)]
        pltpu.make_async_copy(half, half, ps_r.at[o]).wait()
        sm[...] += jnp.dot(fb[g], pb[g, :, HID:], preferred_element_type=F32)
    selfb[...] = sm[...].astype(BF)
    for o in range(1, NY):
        pltpu.make_async_copy(lr.at[o], lr.at[o], l_r.at[o]).wait()

    def zf_copy(t):
        return remote(ms.at[t], zr.at[t], zf_s.at[t], zf_r.at[t], to_yz(y, far_first(t)))

    def merge(t, carry):
        zz = far_first(t)
        for o in range(1, NY):
            pltpu.make_async_copy(yr.at[t, o], yr.at[t, o], yf_r.at[t, o]).wait()

        def rows(n, inner):
            part = pl.ds(pl.multiple_of(n * 32, 32), 32)
            sums = [jnp.zeros((32, HID), F32) for b in range(NB)]
            for o in range(NY):
                for i in range(CAP):
                    row = jnp.broadcast_to(lr[o, pl.ds(zz * CAP + i, 1), :], (32, HID))
                    value = yr[t, o, i, part, :].astype(F32)
                    for b in range(NB):
                        sums[b] = sums[b] + jnp.where(row == b, value, 0.0)
            for b in range(NB):
                ms[t, b, part, :] = sums[b].astype(BF)
            return inner

        lax.fori_loop(0, BLK // 32, rows, 0)

        @pl.when(t < NZ - 1)
        def _():
            zf_copy(t).start()

        def turn(n, inner):
            s = t * (SLOTS // NZ) + n
            for k in range(KB):
                ttb[s, pl.ds(k * BLK, BLK), :] = tb[s, k].T
            return inner

        lax.fori_loop(0, SLOTS // NZ, turn, 0)
        for b in range(NB):
            ftb[t, :, pl.ds(b * BLK, BLK)] = fb[t, pl.ds(b * BLK, BLK), :].T
        return carry

    lax.fori_loop(0, NZ, merge, 0)
    own_g.wait()

    def from_own(b, carry):
        rows = pl.ds(pl.multiple_of(b * BLK, BLK), BLK)
        sm[rows, :] = ms[NZ - 1, b].astype(F32)
        return carry

    lax.fori_loop(0, NB, from_own, 0)

    def gather_z(t, carry):
        pltpu.make_async_copy(zr.at[t], zr.at[t], zf_r.at[t]).wait()

        def add(b, inner):
            rows = pl.ds(pl.multiple_of(b * BLK, BLK), BLK)
            sm[rows, :] = sm[rows, :] + zr[t, b].astype(F32)
            return inner

        lax.fori_loop(0, NB, add, 0)
        return carry

    lax.fori_loop(0, NZ - 1, gather_z, 0)

    def pointwise(n, carry):
        rows = pl.ds(pl.multiple_of(n * 32, 32), 32)
        inv = inv_deg[rows, :]
        preact = sm[rows, :] * inv + selfb[rows, :].astype(F32)
        sigma = jax.nn.sigmoid(preact)
        act_out[rows, :] = (preact * sigma).astype(BF)
        grad_pre = ogb[rows, :].astype(F32) * sigma * (1.0 + preact * (1.0 - sigma))
        gs[rows, :] = grad_pre.astype(BF)
        block = n // (BLK // 32)
        ga[0, block, pl.ds(pl.multiple_of((n % (BLK // 32)) * 32, 32), 32), :] = (
            grad_pre * inv
        ).astype(BF)
        return carry

    lax.fori_loop(0, ROWS // 32, pointwise, 0)

    up, down = to_yz(y, (z + 1) % NZ), to_yz(y, (z + NZ - 1) % NZ)

    def ag_first(way):
        return remote(ga.at[0], ga.at[1 + way], ag_s.at[way], ag_r.at[way], (up, down)[way])

    def ag_next(k, way):
        q = 2 * k - 1 + way
        return remote(
            ga.at[q], ga.at[q + 2], ag_s.at[2 * k + way], ag_r.at[2 * k + way], (up, down)[way]
        )

    def ag_last(way):
        q = NZ - 3 + way
        half = pl.ds(2 * way, 2)
        return remote(
            ga.at[q, half], ga.at[NZ - 1, half], ag_s.at[6 + way], ag_r.at[6 + way], (up, down)[way]
        )

    def yb_copy(q, o):
        return remote(
            bs.at[q, o], br.at[q, NY - o], yb_s.at[q, o], yb_r.at[q, NY - o], to_yz((y + o) % NY, z)
        )

    def answer(q):
        zz = near_first(q)

        def rows(n, inner):
            part = pl.ds(pl.multiple_of(n * 32, 32), 32)
            blocks = [ga[q, b, part, :].astype(F32) for b in range(NB)]
            for o in range(NY):
                for i in range(CAP):
                    row = jnp.broadcast_to(lr[o, pl.ds(zz * CAP + i, 1), :], (32, HID))
                    value = jnp.zeros((32, HID), F32)
                    for b in range(NB):
                        value = jnp.where(row == b, blocks[b], value)
                    if o:
                        bs[q, o, i, part, :] = value.astype(BF)
                    else:
                        br[q, 0, i, part, :] = value.astype(BF)
            return inner

        lax.fori_loop(0, BLK // 32, rows, 0)
        for o in range(1, NY):
            yb_copy(q, o).start()

    def backward(q):
        zz = near_first(q)
        for o in range(1, NY):
            pltpu.make_async_copy(br.at[q, o], br.at[q, o], yb_r.at[q, o]).wait()

        def one(j, carry):
            o, i = j // CAP, j % CAP
            p = (((y + o) % NY) * NZ + zz) * CAP + i
            prod[...] = jnp.dot(ttb[idx[p]], br[q, o, i], preferred_element_type=F32)
            keep = [
                [jnp.where(src[p * KB + k] == b, 1.0, 0.0).astype(F32) for b in range(NB)]
                for k in range(KB)
            ]

            def rows(n, inner):
                base = pl.multiple_of(n * 16, 16)
                parts = [prod[pl.ds(k * BLK + base, 16), :] for k in range(KB)]
                for b in range(NB):
                    total = gacc[b, pl.ds(base, 16), :]
                    for k in range(KB):
                        total = total + keep[k][b] * parts[k]
                    gacc[b, pl.ds(base, 16), :] = total
                return inner

            lax.fori_loop(0, BLK // 16, rows, 0)
            return carry

        lax.fori_loop(0, NY * CAP, one, 0)

    def rc_copy(h):
        return remote(pw.at[h, 1 - c], rc.at[h], rc_s.at[h], rc_r.at[h], to_feat(x * NC + 1 - c))

    def rx_copy(h, o):
        xx = (x + o) % NX
        return remote(
            x1.at[h, xx], rx.at[h, NX - o], rx_s.at[h, o], rx_r.at[h, NX - o], to_feat(xx * NC + c)
        )

    def ry_copy(h, o):
        yy = (y + o) % NY
        return remote(
            y1.at[h, yy], ry.at[h, NY - o], ry_s.at[h, o], ry_r.at[h, NY - o], to_yz(yy, z)
        )

    def rz_copy(h, o):
        zz = (z + o) % NZ
        return remote(
            z1.at[h, zz], rz.at[h, NZ - o], rz_s.at[h, o], rz_r.at[h, NZ - o], to_yz(y, zz)
        )

    def zg_copy(h, o):
        zz = (z + o) % NZ
        return remote(
            zt.at[h], zg.at[h, NZ - o], zg_s.at[h, o], zg_r.at[h, NZ - o], to_yz(y, zz)
        )

    def yg_copy(h, o):
        yy = (y + o) % NY
        return remote(
            yt.at[h], yg.at[h, NY - o], yg_s.at[h, o], yg_r.at[h, NY - o], to_yz(yy, z)
        )

    def red_0(h, grad):
        for g in range(NF):
            pw[h, g % NC, g // NC] = jnp.dot(ftb[g], grad, preferred_element_type=F32)
        rc_copy(h).start()

    def red_1(h):
        rc_copy(h).wait_recv()
        for o in range(1, NX + 1):
            xx = (x + o) % NX
            x1[h, xx] = pw[h, c, xx] + rc[h, xx]
            if o < NX:
                rx_copy(h, o).start()

    def red_2(h):
        total = x1[h, x]
        for o in range(1, NX):
            pltpu.make_async_copy(rx.at[h, o], rx.at[h, o], rx_r.at[h, o]).wait()
            total = total + rx[h, o]
        y1[h] = total.reshape(NY, BLK // NY, HID)
        for o in range(1, NY):
            ry_copy(h, o).start()

    def red_3(h):
        total = y1[h, y]
        for o in range(1, NY):
            pltpu.make_async_copy(ry.at[h, o], ry.at[h, o], ry_r.at[h, o]).wait()
            total = total + ry[h, o]
        for n in range(NZ):
            r, q = n // 2, n % 2
            z1[h, n] = total[r * 8 : r * 8 + 8, q * 128 : q * 128 + 128]
        for o in range(1, NZ):
            rz_copy(h, o).start()

    def red_4(h):
        total = z1[h, z]
        for o in range(1, NZ):
            pltpu.make_async_copy(rz.at[h, o], rz.at[h, o], rz_r.at[h, o]).wait()
            total = total + rz[h, o]
        zt[h] = total
        zg[h, 0] = total
        for o in range(1, NZ):
            zg_copy(h, o).start()

    def red_5(h):
        for o in range(1, NZ):
            pltpu.make_async_copy(zg.at[h, o], zg.at[h, o], zg_r.at[h, o]).wait()
        for n in range(NZ):
            r, q = n // 2, n % 2
            yt[h, pl.ds(r * 8, 8), pl.ds(q * 128, 128)] = zg[h, (n - z + NZ) % NZ]
        for o in range(1, NY):
            yg_copy(h, o).start()

    def red_6(h):
        cols = pl.ds(HID * (1 - h), HID)
        wg_out[pl.ds(pl.multiple_of(y * (BLK // NY), BLK // NY), BLK // NY), cols] = yt[h]
        for o in range(1, NY):
            pltpu.make_async_copy(yg.at[h, o], yg.at[h, o], yg_r.at[h, o]).wait()
            rows = pl.ds(pl.multiple_of(((y + o) % NY) * (BLK // NY), BLK // NY), BLK // NY)
            wg_out[rows, cols] = yg[h, o]

    gacc[...] = jnp.zeros_like(gacc)
    ag_first(0).start()
    ag_first(1).start()
    answer(0)
    red_0(0, gs[...])
    ag_first(0).wait_recv()
    ag_first(1).wait_recv()
    ag_next(1, 0).start()
    ag_next(1, 1).start()
    answer(1)
    answer(2)
    red_1(0)
    ag_next(1, 0).wait_recv()
    ag_next(1, 1).wait_recv()
    ag_next(2, 0).start()
    ag_next(2, 1).start()
    answer(3)
    answer(4)
    red_2(0)
    backward(0)
    ag_next(2, 0).wait_recv()
    ag_next(2, 1).wait_recv()
    ag_last(0).start()
    ag_last(1).start()
    answer(5)
    answer(6)
    red_3(0)
    backward(1)
    ag_last(0).wait_recv()
    ag_last(1).wait_recv()
    answer(7)
    red_4(0)
    backward(2)
    red_5(0)
    backward(3)
    red_6(0)
    for q in range(4, NZ):
        backward(q)

    grad = gacc[...].astype(BF).reshape(ROWS, HID)
    red_0(1, grad)
    for step in (red_1, red_2, red_3, red_4, red_5, red_6):
        step(1)

    for o in range(1, NF):
        f_copy(o).wait_send()
        p_copy(o, 0, pn_s, pn_r).wait_send()
        p_copy(o, 1, ps_s, ps_r).wait_send()
    for o in range(1, NY):
        l_copy(o).wait_send()
    for t in range(NZ):
        for o in range(1, NY):
            yf_copy(t, o).wait_send()
            yb_copy(t, o).wait_send()
        if t < NZ - 1:
            zf_copy(t).wait_send()
    for way in range(2):
        ag_first(way).wait_send()
        ag_next(1, way).wait_send()
        ag_next(2, way).wait_send()
        ag_last(way).wait_send()
    for h in range(2):
        rc_copy(h).wait_send()
        for o in range(1, NX):
            rx_copy(h, o).wait_send()
        for o in range(1, NY):
            ry_copy(h, o).wait_send()
            yg_copy(h, o).wait_send()
        for o in range(1, NZ):
            rz_copy(h, o).wait_send()
            zg_copy(h, o).wait_send()


def local(feats, projection, tiles, slot_owner, slot_block, source_block, counts, out_grad):
    smem = pl.BlockSpec(memory_space=pltpu.SMEM)
    vmem = pl.BlockSpec(memory_space=pltpu.VMEM)
    hbm = pl.BlockSpec(memory_space=pl.ANY)
    places = NY * NZ * CAP
    idx, lab, src = pl.pallas_call(
        table_kernel,
        out_shape=(
            jax.ShapeDtypeStruct((places,), jnp.int32),
            jax.ShapeDtypeStruct((places,), jnp.int32),
            jax.ShapeDtypeStruct((places * KB,), jnp.int32),
        ),
        in_specs=[smem] * 3,
        out_specs=[smem] * 3,
        scratch_shapes=[pltpu.SMEM((NY * NZ,), jnp.int32)],
    )(slot_owner.reshape(-1), slot_block.reshape(-1), source_block.reshape(-1))
    inv_deg = jnp.broadcast_to((1.0 / counts.astype(F32))[:, None], (ROWS, HID))

    dma = pltpu.SemaphoreType.DMA
    scratch = [
        pltpu.VMEM((NF, ROWS, BLK), BF),
        pltpu.VMEM((NF, BLK, 2 * HID), BF),
        pltpu.VMEM((SLOTS, KB, BLK, BLK), BF),
        pltpu.VMEM((ROWS, HID), BF),
        pltpu.VMEM((NB, BLK, HID), BF),
        pltpu.VMEM((ROWS, HID), BF),
        pltpu.VMEM((NF, BLK, ROWS), BF),
        pltpu.VMEM((SLOTS, KB * BLK, BLK), BF),
        pltpu.VMEM((NY, NZ * CAP, HID), jnp.int32),
        pltpu.VMEM((NY, NZ * CAP, HID), jnp.int32),
        pltpu.VMEM((NZ, NY, CAP, BLK, HID), BF),
        pltpu.VMEM((NZ, NY, CAP, BLK, HID), BF),
        pltpu.VMEM((NZ, NB, BLK, HID), BF),
        pltpu.VMEM((NZ, NB, BLK, HID), BF),
        pltpu.VMEM((ROWS, HID), F32),
        pltpu.VMEM((NZ, NB, BLK, HID), BF),
        pltpu.VMEM((NZ, NY, CAP, BLK, HID), BF),
        pltpu.VMEM((NZ, NY, CAP, BLK, HID), BF),
        pltpu.VMEM((ROWS, HID), BF),
        pltpu.VMEM((NB, BLK, HID), F32),
        pltpu.VMEM((KB * BLK, HID), F32),
        pltpu.VMEM((2, NC, NX, BLK, HID), F32),
        pltpu.VMEM((2, NX, BLK, HID), F32),
        pltpu.VMEM((2, NX, BLK, HID), F32),
        pltpu.VMEM((2, NX, BLK, HID), F32),
        pltpu.VMEM((2, NY, BLK // NY, HID), F32),
        pltpu.VMEM((2, NY, BLK // NY, HID), F32),
        pltpu.VMEM((2, NZ, 8, 128), F32),
        pltpu.VMEM((2, NZ, 8, 128), F32),
        pltpu.VMEM((2, 8, 128), F32),
        pltpu.VMEM((2, NZ, 8, 128), F32),
        pltpu.VMEM((2, BLK // NY, HID), F32),
        pltpu.VMEM((2, NY, BLK // NY, HID), F32),
        dma((4,)),
        dma((NF,)), dma((NF,)), dma((NF,)), dma((NF,)), dma((NF,)), dma((NF,)),
        dma((NY,)), dma((NY,)),
        dma((NZ, NY)), dma((NZ, NY)), dma((NZ,)), dma((NZ,)), dma((NZ,)), dma((NZ,)),
        dma((NZ, NY)), dma((NZ, NY)),
        dma((2,)), dma((2,)), dma((2, NX)), dma((2, NX)), dma((2, NY)), dma((2, NY)),
        dma((2, NZ)), dma((2, NZ)), dma((2, NZ)), dma((2, NZ)), dma((2, NY)), dma((2, NY)),
    ]
    return pl.pallas_call(
        main_kernel,
        out_shape=(
            jax.ShapeDtypeStruct((ROWS, HID), BF),
            jax.ShapeDtypeStruct((BLK, 2 * HID), F32),
        ),
        in_specs=[smem] * 3 + [hbm] * 4 + [vmem],
        out_specs=[vmem] * 2,
        scratch_shapes=scratch,
        compiler_params=pltpu.CompilerParams(
            collective_id=0, has_side_effects=True, vmem_limit_bytes=60 << 20
        ),
    )(idx, lab, src, feats.reshape(NF, ROWS, BLK), projection, tiles, out_grad, inv_deg)


def solution(mesh):
    placed = (
        P("dom", "feat"),
        P("feat", None),
        P(("dom", "feat"), None, None, None),
        P(("dom", "feat"), None),
        P(("dom", "feat"), None),
        P(("dom", "feat"), None),
        P(("dom", "feat")),
        P(("dom", "feat"), None),
    )
    return jax.shard_map(
        local,
        mesh=mesh,
        in_specs=placed,
        out_specs=(P(("dom", "feat"), None), P("feat", None)),
        check_vma=False,
    )
```

time: 572 us -> 193 us (0.34)
  waiting for transfers between devices: 405 us -> 0 us
  Pallas kernels: 0 us -> 185 us
  local copies, waits for them, and re-layouts: 64.1 us -> 5.64 us
  matrix products: 47.8 us -> 0 us
  starting transfers between devices: 31.3 us -> 0 us
  between operations: 13.9 us -> 0.65 us
    all_to_all x3 -> x0, waiting for transfers between devices: 185 us -> none  [the longest x1 93.5 us: local(): lax.all_to_all(sending_back, 'dom', split_axis=0, concat_axis=0, tiled=True)]
    pallas_call x0 -> x2, Pallas kernels: none -> 185 us  [the longest x1 182 us: local(): pl.pallas_call(main_kernel, out_shape=(jax.ShapeDtypeStruct((ROWS, HID),...]
    psum x1 -> x0, waiting for transfers between devices: 139 us -> none  [local(): weight_grad = lax.psum(partial_grad, 'dom')]
    dot_general x9 -> x0, matrix products: 47.8 us -> none  [the longest x1 9.02 us: local(): jnp.einsum('bn,njh->bjh', source_hot, flat_products, precision=lax.Precis...]
    reshape x7 -> x1, local copies, waits for them, and re-layouts: 48 us -> 0.62 us  [local(): source_block.reshape(-1)]
    reduce_scatter x1 -> x0, waiting for transfers between devices: 44.3 us -> none  [local(): lax.psum_scatter(jnp.dot(feats, projection, preferred_element_type=jnp.fl...]
    all_gather x1 -> x0, waiting for transfers between devices: 36.3 us -> none  [local(): lax.all_gather(grad_proj, 'feat', axis=0, tiled=True)]
    all_to_all x3 -> x0, starting transfers between devices: 31.2 us -> none  [the longest x1 12 us: local(): lax.all_to_all(labels, 'dom', split_axis=0, concat_axis=0, tiled=True)]
  transfers between devices with their start and end apart: 6 -> 0, of which waited for: 5 -> 0; matrix products, arithmetic and copies ran while one was open for 6% -> 0% of each run, Pallas kernels for 0% -> 0%
where the time goes in v1:
time: 193 us; the launch traced here: 192 us
  Pallas kernels  185 us (96%)
  local copies, waits for them, and re-layouts  5.64 us (3%)
    pallas_call x1, Pallas kernels, local(): pl.pallas_call(main_kernel, out_shape=(jax.ShapeDtypeStruct((ROWS, HID),...  182 us
    unnamed x3, local copies, waits for them, and re-layouts  4.11 us

profile of v1, /device:TPU:1, one launch (start us, length us, event | category | flops | bytes accessed | tf_op | source)
XLA Modules:
  0.0 192.0 jit_solution(3584059086171242196)
XLA Ops:
  0.6 0.7 convert_divide_fusion
  1.3 0.8 copy.11
  2.1 0.6 reshape.19.source_ref
  2.7 2.6 %shard_map.95 = (s32[64]{0:T(128)}, s32[64]{0:T(128)}, s32[256]{0:T(256)}) custom-call(s32[32]{0:T(128)} %bitcast.4, s32[32]{0:T(128)} %bitcast.5, s32[128]{0:T(128)} %reshape.19.source_ref), custom_call_target="tpu_custom_call" | custom-call | tf_op jit(solution)/shard_map/pallas_call | solution.py:508
  5.3 0.9 broadcast_in_dim.2.inv_deg
  6.2 182.5 %shard_map.96 = (bf16[512,256]{1,0:T(8,128)(2,1)}, f32[128,512]{1,0:T(8,128)}) custom-call(s32[64]{0:T(128)} %get-tuple-element.5.idx, s32[64]{0:T(128)} %get-tuple-element.6.lab, s32[256]{0:T(256)} %get-tuple-element.7.src, bf16[8,512,128]{2,1,0:T(8,128)(2,1)} %bitcast.3, bf16[128,512]{1,0:T(8,128)(2,1)} %proj.1, bf16[32,4,128,128]{3,2,1,0:T(8,128)(2,1)} %tiles.1, ...), custom_call_target="tpu_custom_call" | custom-call | tf_op jit(solution)/shard_map/pallas_call | solution.py:564
  188.7 1.7 copy.14
  190.4 1.7 copy.15

commit v2 on v1

v2 whole, which is shorter than its diff:
```python
import jax
import jax.numpy as jnp
from jax import lax
from jax.experimental import pallas as pl
from jax.experimental.pallas import tpu as pltpu
from jax.sharding import PartitionSpec as P

MESH = pl.DeviceIdType.MESH
NY, NZ, NX, NC = 4, 8, 4, 2
NF = NX * NC
ND = NY * NZ
FAR_FIRST = ((2, 0), (2, 1), (1, 0), (3, 0), (1, 1), (3, 1), (0, 1))
NEAR_FIRST = FAR_FIRST[::-1]
BLK = 128
NB = 4
HID = 256
ROWS = NB * BLK
KB = 4
SLOTS = 32
CAP = 2
BF, F32 = jnp.bfloat16, jnp.float32


def main_kernel(
    owner, block, source, counts, feats, proj, tiles, out_grad,
    act_out, wg_out,
    fb, pb, tb, ogb, nb, selfb, ftb, wt, tabv, tabs, inv_deg,
    ls, lr, cs, yr, ms, zr, sm,
    ga, bs, br, gs, gacc,
    pw, rc, x1, rx, y1, ry, yt, yg,
    loc_sem, f_s, f_r, px_s, px_r, py_s, py_r, pc_s, pc_r, l_s, l_r,
    yf_s, yf_r, zf_s, zf_r, ag_s, ag_r, yb_s, yb_r,
    rc_s, rc_r, rx_s, rx_r, ry_s, ry_r, yg_s, yg_r,
):
    d = lax.axis_index("dom")
    f = lax.axis_index("feat")
    y, z = d // NZ, d % NZ
    x, c = f // NC, f % NC

    def to_feat(g):
        return (d, g)

    def to_yz(yy, zz):
        return (yy * NZ + zz, f)

    def remote(a, b, s, r, dev):
        return pltpu.make_async_remote_copy(
            src_ref=a, dst_ref=b, send_sem=s, recv_sem=r, device_id=dev, device_id_type=MESH
        )

    own_f = pltpu.make_async_copy(feats.at[f], fb.at[f], loc_sem.at[0])
    own_p = pltpu.make_async_copy(proj, pb.at[x, c], loc_sem.at[1])
    own_t = pltpu.make_async_copy(tiles, tb, loc_sem.at[2])
    own_g = pltpu.make_async_copy(out_grad, ogb, loc_sem.at[3])
    own_f.start()
    own_p.start()

    barrier = pltpu.get_barrier_semaphore()
    for o in range(1, NF):
        pl.semaphore_signal(barrier, inc=1, device_id=to_feat((f + o) % NF), device_id_type=MESH)
    for o in range(1, ND):
        pl.semaphore_signal(barrier, inc=1, device_id=((d + o) % ND, f), device_id_type=MESH)
    pl.semaphore_wait(barrier, NF + ND - 2)

    def f_copy(ox, oc):
        g = ((x + ox) % NX) * NC + (c + oc) % NC
        back = ((NX - ox) % NX) * NC + oc
        return remote(feats.at[g], fb.at[f], f_s.at[ox * NC + oc], f_r.at[back], to_feat(g))

    sibling = to_feat(x * NC + 1 - c)
    quarter = pl.ds(pl.multiple_of(y * (BLK // NY), BLK // NY), BLK // NY)

    def px_copy(o):
        return remote(
            proj.at[quarter], pb.at[x, c, quarter], px_s.at[o], px_r.at[NX - o],
            to_feat(((x + o) % NX) * NC + c),
        )

    def py_copy(o, oy):
        piece = pb.at[(x + o) % NX, c, quarter]
        return remote(
            piece, piece, py_s.at[o, oy], py_r.at[o, NY - oy], to_yz((y + oy) % NY, z)
        )

    def pc_copy(o):
        shard = pb.at[(x + o) % NX, c]
        return remote(shard if o else proj, shard, pc_s.at[o], pc_r.at[o], sibling)

    for o in (2, 1, 3):
        px_copy(o).start()
    for ox, oc in FAR_FIRST:
        f_copy(ox, oc).start()
    pc_copy(0).start()
    own_t.start()
    own_g.start()

    o_at = lax.broadcasted_iota(jnp.int32, (ND, SLOTS), 0)
    s_at = lax.broadcasted_iota(jnp.int32, (ND, SLOTS), 1)
    named = owner[...] == o_at
    before = jnp.dot(
        named.astype(BF), (o_at < s_at).astype(BF), preferred_element_type=F32
    )
    lane = lax.broadcasted_iota(jnp.int32, (ND, 128), 1)
    for i in range(CAP):
        here = named & (before == float(i))
        slot = jnp.sum(jnp.where(here, s_at.astype(F32), 0.0), axis=1, keepdims=True)
        label = jnp.sum(
            jnp.where(here, block[...].astype(F32) + 1.0, 0.0), axis=1, keepdims=True
        )
        tabv[i] = jnp.where(lane == 0, slot, 0.0).astype(jnp.int32)
        rows = jnp.broadcast_to((label - 1.0).astype(jnp.int32), (ND, HID))
        ls[:, i] = rows.reshape(NY, NZ, HID)
    picks = jnp.zeros((SLOTS, 128), F32)
    for k in range(KB):
        column = jnp.sum(
            jnp.where(o_at == s_at, source[k : k + 1, :].astype(F32), 0.0), axis=1, keepdims=True
        )
        picks = picks + jnp.where(lane == k, column, 0.0)
    tabv[CAP] = picks.astype(jnp.int32)
    table = pltpu.make_async_copy(tabv, tabs, loc_sem.at[4])
    table.start()

    def l_copy(o):
        yy = (y + o) % NY
        return remote(ls.at[yy], lr.at[NY - o], l_s.at[o], l_r.at[NY - o], to_yz(yy, z))

    for o in range(1, NY):
        l_copy(o).start()
    lr[0] = ls[y]

    for o in (1, 3, 2):
        piece = pb.at[(x + o) % NX, c, quarter]
        pltpu.make_async_copy(piece, piece, px_r.at[o]).wait()
        for oy in range(1, NY):
            py_copy(o, oy).start()

    diagonal = lax.broadcasted_iota(jnp.int32, (BLK, BLK), 0) == lax.broadcasted_iota(
        jnp.int32, (BLK, BLK), 1
    )
    for b in range(NB):
        column = jnp.sum(
            jnp.where(diagonal, counts[b : b + 1, :].astype(F32), 0.0), axis=1, keepdims=True
        )
        inv_deg[b * BLK : (b + 1) * BLK, :] = jnp.broadcast_to(1.0 / column, (BLK, HID))

    own_p.wait()
    for o in (1, 3, 2):
        for oy in range(1, NY):
            theirs = pl.ds(pl.multiple_of(((y + oy) % NY) * (BLK // NY), BLK // NY), BLK // NY)
            piece = pb.at[(x + o) % NX, c, theirs]
            pltpu.make_async_copy(piece, piece, py_r.at[o, oy]).wait()
        pc_copy(o).start()
    table.wait()

    own_f.wait()
    for o in range(NX):
        shard = pb.at[(x + o) % NX, 1 - c]
        pltpu.make_async_copy(shard, shard, pc_r.at[o]).wait()
    sm[...] = jnp.dot(fb[f], pb[x, c, :, :HID], preferred_element_type=F32)
    for ox, oc in NEAR_FIRST:
        xx, cc = (x + ox) % NX, (c + oc) % NC
        g = xx * NC + cc
        pltpu.make_async_copy(fb.at[g], fb.at[g], f_r.at[ox * NC + oc]).wait()
        sm[...] += jnp.dot(fb[g], pb[xx, cc, :, :HID], preferred_element_type=F32)
    nb[...] = sm[...].astype(BF).reshape(NB, BLK, HID)
    own_t.wait()

    def far_first(t):
        return (z + NZ // 2 + (1 - 2 * (t % 2)) * ((t + 1) // 2)) % NZ

    def near_first(q):
        return (z + NZ + (1 - 2 * (q % 2)) * ((q + 1) // 2)) % NZ

    def yf_copy(t, o):
        return remote(
            cs.at[t, o], yr.at[t, NY - o], yf_s.at[t, o], yf_r.at[t, NY - o], to_yz((y + o) % NY, z)
        )

    def slot_at(i, at):
        return jnp.clip(tabs[i, at, 0], 0, SLOTS - 1)

    def source_at(s, k):
        return jnp.clip(tabs[CAP, s, k], 0, NB - 1)

    def contribute(t, carry):
        zz = far_first(t)
        for o in range(1, NY + 1):
            r = o % NY
            yy = (y + r) % NY
            for i in range(CAP):
                s = slot_at(i, yy * NZ + zz)
                total = None
                for k in range(0, KB, 2):
                    left = jnp.concatenate([tb[s, k], tb[s, k + 1]], axis=1)
                    right = jnp.concatenate(
                        [nb[source_at(s, k)], nb[source_at(s, k + 1)]], axis=0
                    )
                    part = jnp.dot(left, right, preferred_element_type=F32)
                    total = part if total is None else total + part
                if r:
                    cs[t, r, i] = total.astype(BF)
                else:
                    yr[t, 0, i] = total.astype(BF)
            if r:
                yf_copy(t, r).start()
        return carry

    lax.fori_loop(0, NZ, contribute, 0)

    sm[...] = jnp.dot(fb[f], pb[x, c, :, HID:], preferred_element_type=F32)
    for ox, oc in NEAR_FIRST:
        xx, cc = (x + ox) % NX, (c + oc) % NC
        sm[...] += jnp.dot(fb[xx * NC + cc], pb[xx, cc, :, HID:], preferred_element_type=F32)
    selfb[...] = sm[...].astype(BF)
    for o in range(1, NY):
        pltpu.make_async_copy(lr.at[o], lr.at[o], l_r.at[o]).wait()

    def zf_copy(t):
        return remote(ms.at[t], zr.at[t], zf_s.at[t], zf_r.at[t], to_yz(y, far_first(t)))

    def merge(t, carry):
        zz = far_first(t)
        for o in range(1, NY):
            pltpu.make_async_copy(yr.at[t, o], yr.at[t, o], yf_r.at[t, o]).wait()

        def rows(n, inner):
            part = pl.ds(pl.multiple_of(n * 32, 32), 32)
            sums = [jnp.zeros((32, HID), F32) for b in range(NB)]
            for o in range(NY):
                for i in range(CAP):
                    row = jnp.broadcast_to(lr[o, i, pl.ds(zz, 1), :], (32, HID))
                    value = yr[t, o, i, part, :].astype(F32)
                    for b in range(NB):
                        sums[b] = sums[b] + jnp.where(row == b, value, 0.0)
            for b in range(NB):
                ms[t, b, part, :] = sums[b].astype(BF)
            return inner

        lax.fori_loop(0, BLK // 32, rows, 0)

        @pl.when(t < NZ - 1)
        def _():
            zf_copy(t).start()

        def turn(n, inner):
            s = t * (SLOTS // NZ) + n
            parts = [tb[s, k].astype(F32) for k in range(KB)]
            for b in range(NB):
                total = jnp.zeros((BLK, BLK), F32)
                for k in range(KB):
                    total = total + jnp.where(source_at(s, k) == b, parts[k], 0.0)
                wt[s, pl.ds(b * BLK, BLK), :] = total.astype(BF).T
            return inner

        lax.fori_loop(0, SLOTS // NZ, turn, 0)
        for b in range(NB):
            ftb[t, :, pl.ds(b * BLK, BLK)] = fb[t, pl.ds(b * BLK, BLK), :].T
        return carry

    lax.fori_loop(0, NZ, merge, 0)
    own_g.wait()

    def from_own(b, carry):
        rows = pl.ds(pl.multiple_of(b * BLK, BLK), BLK)
        sm[rows, :] = ms[NZ - 1, b].astype(F32)
        return carry

    lax.fori_loop(0, NB, from_own, 0)

    def gather_z(t, carry):
        pltpu.make_async_copy(zr.at[t], zr.at[t], zf_r.at[t]).wait()

        def add(b, inner):
            rows = pl.ds(pl.multiple_of(b * BLK, BLK), BLK)
            sm[rows, :] = sm[rows, :] + zr[t, b].astype(F32)
            return inner

        lax.fori_loop(0, NB, add, 0)
        return carry

    lax.fori_loop(0, NZ - 1, gather_z, 0)

    def pointwise(n, carry):
        rows = pl.ds(pl.multiple_of(n * 32, 32), 32)
        inv = inv_deg[rows, :]
        preact = sm[rows, :] * inv + selfb[rows, :].astype(F32)
        sigma = jax.nn.sigmoid(preact)
        act_out[rows, :] = (preact * sigma).astype(BF)
        grad_pre = ogb[rows, :].astype(F32) * sigma * (1.0 + preact * (1.0 - sigma))
        gs[rows, :] = grad_pre.astype(BF)
        block = n // (BLK // 32)
        ga[0, block, pl.ds(pl.multiple_of((n % (BLK // 32)) * 32, 32), 32), :] = (
            grad_pre * inv
        ).astype(BF)
        return carry

    lax.fori_loop(0, ROWS // 32, pointwise, 0)

    up, down = to_yz(y, (z + 1) % NZ), to_yz(y, (z + NZ - 1) % NZ)

    def ag_first(way):
        return remote(ga.at[0], ga.at[1 + way], ag_s.at[way], ag_r.at[way], (up, down)[way])

    def ag_next(k, way):
        q = 2 * k - 1 + way
        return remote(
            ga.at[q], ga.at[q + 2], ag_s.at[2 * k + way], ag_r.at[2 * k + way], (up, down)[way]
        )

    def ag_last(way):
        q = NZ - 3 + way
        half = pl.ds(2 * way, 2)
        return remote(
            ga.at[q, half], ga.at[NZ - 1, half], ag_s.at[6 + way], ag_r.at[6 + way], (up, down)[way]
        )

    def yb_copy(q, o):
        return remote(
            bs.at[q, o], br.at[q, NY - o], yb_s.at[q, o], yb_r.at[q, NY - o], to_yz((y + o) % NY, z)
        )

    def answer(q):
        zz = near_first(q)

        def rows(n, inner):
            part = pl.ds(pl.multiple_of(n * 32, 32), 32)
            blocks = [ga[q, b, part, :].astype(F32) for b in range(NB)]
            for o in range(NY):
                for i in range(CAP):
                    row = jnp.broadcast_to(lr[o, i, pl.ds(zz, 1), :], (32, HID))
                    value = jnp.zeros((32, HID), F32)
                    for b in range(NB):
                        value = jnp.where(row == b, blocks[b], value)
                    if o:
                        bs[q, o, i, part, :] = value.astype(BF)
                    else:
                        br[q, 0, i, part, :] = value.astype(BF)
            return inner

        lax.fori_loop(0, BLK // 32, rows, 0)
        for o in range(1, NY):
            yb_copy(q, o).start()

    def backward(q):
        zz = near_first(q)
        for o in range(1, NY):
            pltpu.make_async_copy(br.at[q, o], br.at[q, o], yb_r.at[q, o]).wait()

        def pair(r, carry):
            at = ((y + r) % NY) * NZ + zz
            left = jnp.concatenate([wt[slot_at(0, at)], wt[slot_at(1, at)]], axis=1)
            right = br[q, r].reshape(CAP * BLK, HID)
            gacc[...] += jnp.dot(left, right, preferred_element_type=F32)
            return carry

        lax.fori_loop(0, NY, pair, 0)

    def rc_copy(h, o):
        xx = (x + o) % NX
        return remote(pw.at[h, xx], rc.at[h, xx], rc_s.at[h, o], rc_r.at[h, o], sibling)

    def rx_copy(h, o):
        xx = (x + o) % NX
        return remote(
            x1.at[h, xx], rx.at[h, NX - o], rx_s.at[h, o], rx_r.at[h, NX - o], to_feat(xx * NC + c)
        )

    def ry_copy(h, o):
        e = (d + o) % ND
        return remote(y1.at[h, e], ry.at[h, ND - o], ry_s.at[h], ry_r.at[h], (e, f))

    def yg_copy(h, o):
        return remote(yt.at[h], yg.at[h, ND - o], yg_s.at[h], yg_r.at[h], ((d + o) % ND, f))

    def red_0(h, grad):
        for o in (2, 1, 3, 0):
            xx = (x + o) % NX
            pw[h, xx] = jnp.dot(ftb[xx * NC + 1 - c], grad, preferred_element_type=F32)
            rc_copy(h, o).start()
        for o in (2, 1, 3, 0):
            xx = (x + o) % NX
            x1[h, xx] = jnp.dot(ftb[xx * NC + c], grad, preferred_element_type=F32)

    def red_1(h):
        for o in (2, 1, 3, 0):
            xx = (x + o) % NX
            rc_copy(h, o).wait_recv()
            x1[h, xx] = x1[h, xx] + rc[h, xx]
            if o:
                rx_copy(h, o).start()

    def red_2(h):
        total = x1[h, x]
        for o in (1, 3, 2):
            pltpu.make_async_copy(rx.at[h, o], rx.at[h, o], rx_r.at[h, o]).wait()
            total = total + rx[h, o]
        for n in range(ND):
            r, q = n // 2, n % 2
            y1[h, n] = total[r * 8 : r * 8 + 8, q * 128 : q * 128 + 128]

        def send(o, carry):
            ry_copy(h, o).start()
            return carry

        lax.fori_loop(1, ND, send, 0)

    def others(buf, h):
        return buf.at[h, pl.ds(1, ND - 1)]

    def red_3(h):
        total = y1[h, d]
        pltpu.make_async_copy(others(ry, h), others(ry, h), ry_r.at[h]).wait()
        for o in range(1, ND):
            total = total + ry[h, o]
        yt[h] = total
        yg[h, 0] = total

        def send(o, carry):
            yg_copy(h, o).start()
            return carry

        lax.fori_loop(1, ND, send, 0)

    def red_4(h):
        pltpu.make_async_copy(others(yg, h), others(yg, h), yg_r.at[h]).wait()
        for n in range(ND):
            r, q = n // 2, n % 2
            wg_out[pl.ds(r * 8, 8), pl.ds(HID * (1 - h) + q * 128, 128)] = yg[h, (n - d + ND) % ND]

    gacc[...] = jnp.zeros_like(gacc)
    ag_first(0).start()
    ag_first(1).start()
    answer(0)
    red_0(0, gs[...])
    ag_first(0).wait_recv()
    ag_first(1).wait_recv()
    ag_next(1, 0).start()
    ag_next(1, 1).start()
    answer(1)
    answer(2)
    red_1(0)
    ag_next(1, 0).wait_recv()
    ag_next(1, 1).wait_recv()
    ag_next(2, 0).start()
    ag_next(2, 1).start()
    answer(3)
    answer(4)
    red_2(0)
    backward(0)
    ag_next(2, 0).wait_recv()
    ag_next(2, 1).wait_recv()
    ag_last(0).start()
    ag_last(1).start()
    answer(5)
    answer(6)
    red_3(0)
    backward(1)
    ag_last(0).wait_recv()
    ag_last(1).wait_recv()
    answer(7)
    red_4(0)
    backward(2)
    backward(3)
    for q in range(4, NZ):
        backward(q)

    grad = gacc[...].astype(BF)
    red_0(1, grad)
    for step in (red_1, red_2, red_3, red_4):
        step(1)

    for ox, oc in FAR_FIRST:
        f_copy(ox, oc).wait_send()
    for o in range(1, NX):
        px_copy(o).wait_send()
        for oy in range(1, NY):
            py_copy(o, oy).wait_send()
    for o in range(NX):
        pc_copy(o).wait_send()
    for o in range(1, NY):
        l_copy(o).wait_send()
    for t in range(NZ):
        for o in range(1, NY):
            yf_copy(t, o).wait_send()
            yb_copy(t, o).wait_send()
        if t < NZ - 1:
            zf_copy(t).wait_send()
    for way in range(2):
        ag_first(way).wait_send()
        ag_next(1, way).wait_send()
        ag_next(2, way).wait_send()
        ag_last(way).wait_send()
    for h in range(2):
        for o in range(NX):
            rc_copy(h, o).wait_send()
        for o in range(1, NX):
            rx_copy(h, o).wait_send()
        for buf, sem in ((ry, ry_s), (yg, yg_s)):
            pltpu.make_async_copy(others(buf, h), others(buf, h), sem.at[h]).wait()


def local(feats, projection, tiles, slot_owner, slot_block, source_block, counts, out_grad):
    vmem = pl.BlockSpec(memory_space=pltpu.VMEM)
    hbm = pl.BlockSpec(memory_space=pl.ANY)
    dma = pltpu.SemaphoreType.DMA
    scratch = [
        pltpu.VMEM((NF, ROWS, BLK), BF),
        pltpu.VMEM((NX, NC, BLK, 2 * HID), BF),
        pltpu.VMEM((SLOTS, KB, BLK, BLK), BF),
        pltpu.VMEM((ROWS, HID), BF),
        pltpu.VMEM((NB, BLK, HID), BF),
        pltpu.VMEM((ROWS, HID), BF),
        pltpu.VMEM((NF, BLK, ROWS), BF),
        pltpu.VMEM((SLOTS, NB * BLK, BLK), BF),
        pltpu.VMEM((CAP + 1, ND, 128), jnp.int32),
        pltpu.SMEM((CAP + 1, ND, 128), jnp.int32),
        pltpu.VMEM((ROWS, HID), F32),
        pltpu.VMEM((NY, CAP, NZ, HID), jnp.int32),
        pltpu.VMEM((NY, CAP, NZ, HID), jnp.int32),
        pltpu.VMEM((NZ, NY, CAP, BLK, HID), BF),
        pltpu.VMEM((NZ, NY, CAP, BLK, HID), BF),
        pltpu.VMEM((NZ, NB, BLK, HID), BF),
        pltpu.VMEM((NZ, NB, BLK, HID), BF),
        pltpu.VMEM((ROWS, HID), F32),
        pltpu.VMEM((NZ, NB, BLK, HID), BF),
        pltpu.VMEM((NZ, NY, CAP, BLK, HID), BF),
        pltpu.VMEM((NZ, NY, CAP, BLK, HID), BF),
        pltpu.VMEM((ROWS, HID), BF),
        pltpu.VMEM((ROWS, HID), F32),
        pltpu.VMEM((2, NX, BLK, HID), F32),
        pltpu.VMEM((2, NX, BLK, HID), F32),
        pltpu.VMEM((2, NX, BLK, HID), F32),
        pltpu.VMEM((2, NX, BLK, HID), F32),
        pltpu.VMEM((2, ND, 8, 128), F32),
        pltpu.VMEM((2, ND, 8, 128), F32),
        pltpu.VMEM((2, 8, 128), F32),
        pltpu.VMEM((2, ND, 8, 128), F32),
        dma((5,)),
        dma((NF,)), dma((NF,)), dma((NX,)), dma((NX,)), dma((NX, NY)), dma((NX, NY)),
        dma((NX,)), dma((NX,)), dma((NY,)), dma((NY,)),
        dma((NZ, NY)), dma((NZ, NY)), dma((NZ,)), dma((NZ,)), dma((NZ,)), dma((NZ,)),
        dma((NZ, NY)), dma((NZ, NY)),
        dma((2, NX)), dma((2, NX)), dma((2, NX)), dma((2, NX)),
        dma((2,)), dma((2,)), dma((2,)), dma((2,)),
    ]
    return pl.pallas_call(
        main_kernel,
        out_shape=(
            jax.ShapeDtypeStruct((ROWS, HID), BF),
            jax.ShapeDtypeStruct((BLK, 2 * HID), F32),
        ),
        in_specs=[vmem] * 4 + [hbm] * 4,
        out_specs=[vmem] * 2,
        scratch_shapes=scratch,
        compiler_params=pltpu.CompilerParams(
            collective_id=0, has_side_effects=True, vmem_limit_bytes=60 << 20
        ),
    )(
        slot_owner.reshape(1, SLOTS),
        slot_block.reshape(1, SLOTS),
        source_block.T,
        counts.reshape(NB, BLK),
        feats.reshape(NF, ROWS, BLK),
        projection,
        tiles,
        out_grad,
    )


def solution(mesh):
    placed = (
        P("dom", "feat"),
        P("feat", None),
        P(("dom", "feat"), None, None, None),
        P(("dom", "feat"), None),
        P(("dom", "feat"), None),
        P(("dom", "feat"), None),
        P(("dom", "feat")),
        P(("dom", "feat"), None),
    )
    return jax.shard_map(
        local,
        mesh=mesh,
        in_specs=placed,
        out_specs=(P(("dom", "feat"), None), P("feat", None)),
        check_vma=False,
    )
```

time: 193 us -> 170 us (0.88)
  Pallas kernels: 185 us -> 166 us
  local copies, waits for them, and re-layouts: 5.64 us -> 3.34 us
    pallas_call x1, Pallas kernels: 182 us -> 166 us  [local(): pl.pallas_call(main_kernel, out_shape=(jax.ShapeDtypeStruct((ROWS, HID),...]
    pallas_call x1 -> x0, Pallas kernels: 2.57 us -> none  [local(): pl.pallas_call(table_kernel, out_shape=(jax.ShapeDtypeStruct((places,), j...]
    unnamed x3 -> x2, local copies, waits for them, and re-layouts: 4.11 us -> 3.34 us
where the time goes in v2:
time: 170 us
  Pallas kernels  166 us (98%)
  local copies, waits for them, and re-layouts  3.34 us (2%)
    pallas_call x1, Pallas kernels, local(): pl.pallas_call(main_kernel, out_shape=(jax.ShapeDtypeStruct((ROWS, HID),...  166 us

profile of v2, /device:TPU:1, one launch (start us, length us, event | category | flops | bytes accessed | tf_op | source)
XLA Modules:
  0.0 169.9 jit_solution(10759402477694562881)
XLA Ops:
  0.6 165.9 %shard_map.95 = (bf16[512,256]{1,0:T(8,128)(2,1)}, f32[128,512]{1,0:T(8,128)}) custom-call(s32[1,32]{1,0:T(1,128)} %bitcast.8, s32[1,32]{1,0:T(1,128)} %bitcast.9, s32[4,32]{1,0:T(4,128)} %bitcast.6, s32[4,128]{1,0:T(4,128)} %bitcast.7, bf16[8,512,128]{2,1,0:T(8,128)(2,1)} %bitcast.5, bf16[128,512]{1,0:T(8,128)(2,1)} %proj.1, ...), custom_call_target="tpu_custom_call" | custom-call | tf_op jit(solution)/shard_map/pallas_call | solution.py:546
  166.5 1.7 copy.12
  168.2 1.7 copy.13

commit v3 on v2

--- a/solution.py
+++ b/solution.py
@@ -12,6 +12,7 @@
 FAR_FIRST = ((2, 0), (2, 1), (1, 0), (3, 0), (1, 1), (3, 1), (0, 1))
 NEAR_FIRST = FAR_FIRST[::-1]
 BLK = 128
+HALF = 64
 NB = 4
 HID = 256
 ROWS = NB * BLK
@@ -25,11 +26,11 @@
     owner, block, source, counts, feats, proj, tiles, out_grad,
     act_out, wg_out,
     fb, pb, tb, ogb, nb, selfb, ftb, wt, tabv, tabs, inv_deg,
-    ls, lr, cs, yr, ms, zr, sm,
+    ls, lr, cs, yr, ms, zr, zx, zy, sm,
     ga, bs, br, gs, gacc,
     pw, rc, x1, rx, y1, ry, yt, yg,
     loc_sem, f_s, f_r, px_s, px_r, py_s, py_r, pc_s, pc_r, l_s, l_r,
-    yf_s, yf_r, zf_s, zf_r, ag_s, ag_r, yb_s, yb_r,
+    yf_s, yf_r, zf_s, zf_r, zx_s, zx_r, zy_s, zy_r, ag_s, ag_r, yb_s, yb_r,
     rc_s, rc_r, rx_s, rx_r, ry_s, ry_r, yg_s, yg_r,
 ):
     d = lax.axis_index("dom")
@@ -215,13 +216,27 @@
     for o in range(1, NY):
         pltpu.make_async_copy(lr.at[o], lr.at[o], l_r.at[o]).wait()
 
+    def along_z(o):
+        return to_yz(y, (z + o + NZ) % NZ)
+
     def zf_copy(t):
-        return remote(ms.at[t], zr.at[t], zf_s.at[t], zf_r.at[t], to_yz(y, far_first(t)))
-
-    def merge(t, carry):
+        return remote(ms.at[t], zr.at[t], zf_s.at[t], zf_r.at[t], along_z({3: 2, 4: -2, 5: 1, 6: -1}[t]))
+
+    def zx_copy(way):
+        half = ms.at[0, pl.ds(2 * way, 2)]
+        return remote(half, zx.at[way], zx_s.at[way], zx_r.at[way], along_z((2, -2)[way]))
+
+    def zy_copy(way):
+        return remote(ms.at[1 + way], zy.at[way], zy_s.at[way], zy_r.at[way], along_z((1, -1)[way]))
+
+    def merge(t):
         zz = far_first(t)
         for o in range(1, NY):
             pltpu.make_async_copy(yr.at[t, o], yr.at[t, o], yf_r.at[t, o]).wait()
+        way = t - 3
+        if way in (0, 1):
+            zx_copy(way).wait_recv()
+            zy_copy(way).wait_recv()
 
         def rows(n, inner):
             part = pl.ds(pl.multiple_of(n * 32, 32), 32)
@@ -233,17 +248,27 @@
                     for b in range(NB):
                         sums[b] = sums[b] + jnp.where(row == b, value, 0.0)
             for b in range(NB):
-                ms[t, b, part, :] = sums[b].astype(BF)
+                if way in (0, 1):
+                    sums[b] = sums[b] + zy[way, b, part, :].astype(F32)
+                    if b // 2 == way:
+                        sums[b] = sums[b] + zx[way, b % 2, part, :].astype(F32)
+                if t < NZ - 1:
+                    ms[t, b, part, :] = sums[b].astype(BF)
+                else:
+                    sm[pl.ds(pl.multiple_of(b * BLK + n * 32, 32), 32), :] = sums[b]
             return inner
 
         lax.fori_loop(0, BLK // 32, rows, 0)
-
-        @pl.when(t < NZ - 1)
-        def _():
+        if t == 0:
+            zx_copy(0).start()
+            zx_copy(1).start()
+        elif t < 3:
+            zy_copy(t - 1).start()
+        elif t < NZ - 1:
             zf_copy(t).start()
 
         def turn(n, inner):
-            s = t * (SLOTS // NZ) + n
+            s = t * (SLOTS // (NZ - 1)) + n
             parts = [tb[s, k].astype(F32) for k in range(KB)]
             for b in range(NB):
                 total = jnp.zeros((BLK, BLK), F32)
@@ -252,22 +277,18 @@
                 wt[s, pl.ds(b * BLK, BLK), :] = total.astype(BF).T
             return inner
 
-        lax.fori_loop(0, SLOTS // NZ, turn, 0)
-        for b in range(NB):
-            ftb[t, :, pl.ds(b * BLK, BLK)] = fb[t, pl.ds(b * BLK, BLK), :].T
-        return carry
-
-    lax.fori_loop(0, NZ, merge, 0)
+        if t < NZ - 1:
+            most = SLOTS // (NZ - 1)
+            lax.fori_loop(0, most if t < NZ - 2 else SLOTS - t * most, turn, 0)
+            for g in (t, NZ - 1) if t == NZ - 2 else (t,):
+                for b in range(NB):
+                    ftb[g, :, pl.ds(b * BLK, BLK)] = fb[g, pl.ds(b * BLK, BLK), :].T
+
+    for t in range(NZ):
+        merge(t)
     own_g.wait()
 
-    def from_own(b, carry):
-        rows = pl.ds(pl.multiple_of(b * BLK, BLK), BLK)
-        sm[rows, :] = ms[NZ - 1, b].astype(F32)
-        return carry
-
-    lax.fori_loop(0, NB, from_own, 0)
-
-    def gather_z(t, carry):
+    for t in range(3, NZ - 1):
         pltpu.make_async_copy(zr.at[t], zr.at[t], zf_r.at[t]).wait()
 
         def add(b, inner):
@@ -276,55 +297,45 @@
             return inner
 
         lax.fori_loop(0, NB, add, 0)
-        return carry
-
-    lax.fori_loop(0, NZ - 1, gather_z, 0)
-
-    def pointwise(n, carry):
-        rows = pl.ds(pl.multiple_of(n * 32, 32), 32)
-        inv = inv_deg[rows, :]
-        preact = sm[rows, :] * inv + selfb[rows, :].astype(F32)
-        sigma = jax.nn.sigmoid(preact)
-        act_out[rows, :] = (preact * sigma).astype(BF)
-        grad_pre = ogb[rows, :].astype(F32) * sigma * (1.0 + preact * (1.0 - sigma))
-        gs[rows, :] = grad_pre.astype(BF)
-        block = n // (BLK // 32)
-        ga[0, block, pl.ds(pl.multiple_of((n % (BLK // 32)) * 32, 32), 32), :] = (
-            grad_pre * inv
-        ).astype(BF)
-        return carry
-
-    lax.fori_loop(0, ROWS // 32, pointwise, 0)
+
+    def pointwise(u):
+        def some(n, carry):
+            b, m = n // 2, n % 2
+            rows = pl.ds(pl.multiple_of(b * BLK + u * HALF + m * 32, 32), 32)
+            inv = inv_deg[rows, :]
+            preact = sm[rows, :] * inv + selfb[rows, :].astype(F32)
+            sigma = jax.nn.sigmoid(preact)
+            act_out[rows, :] = (preact * sigma).astype(BF)
+            grad_pre = ogb[rows, :].astype(F32) * sigma * (1.0 + preact * (1.0 - sigma))
+            gs[rows, :] = grad_pre.astype(BF)
+            ga[0, b, u, pl.ds(pl.multiple_of(m * 32, 32), 32), :] = (grad_pre * inv).astype(BF)
+            return carry
+
+        lax.fori_loop(0, NB * 2, some, 0)
 
     up, down = to_yz(y, (z + 1) % NZ), to_yz(y, (z + NZ - 1) % NZ)
 
-    def ag_first(way):
-        return remote(ga.at[0], ga.at[1 + way], ag_s.at[way], ag_r.at[way], (up, down)[way])
-
-    def ag_next(k, way):
-        q = 2 * k - 1 + way
+    def ag_copy(k, way, u):
+        q = 2 * k - 1 + way if k else 0
+        blocks = pl.ds(0, NB) if k < NZ // 2 - 1 else pl.ds(2 * way, 2)
+        to = 2 * k + 1 + way if k < NZ // 2 - 1 else NZ - 1
         return remote(
-            ga.at[q], ga.at[q + 2], ag_s.at[2 * k + way], ag_r.at[2 * k + way], (up, down)[way]
-        )
-
-    def ag_last(way):
-        q = NZ - 3 + way
-        half = pl.ds(2 * way, 2)
+            ga.at[q, blocks, u], ga.at[to, blocks, u],
+            ag_s.at[2 * k + way, u], ag_r.at[2 * k + way, u], (up, down)[way],
+        )
+
+    def yb_copy(q, o, u):
         return remote(
-            ga.at[q, half], ga.at[NZ - 1, half], ag_s.at[6 + way], ag_r.at[6 + way], (up, down)[way]
-        )
-
-    def yb_copy(q, o):
-        return remote(
-            bs.at[q, o], br.at[q, NY - o], yb_s.at[q, o], yb_r.at[q, NY - o], to_yz((y + o) % NY, z)
-        )
-
-    def answer(q):
+            bs.at[q, o, :, u], br.at[q, NY - o, :, u], yb_s.at[q, o, u], yb_r.at[q, NY - o, u],
+            to_yz((y + o) % NY, z),
+        )
+
+    def answer(q, u):
         zz = near_first(q)
 
         def rows(n, inner):
             part = pl.ds(pl.multiple_of(n * 32, 32), 32)
-            blocks = [ga[q, b, part, :].astype(F32) for b in range(NB)]
+            blocks = [ga[q, b, u, part, :].astype(F32) for b in range(NB)]
             for o in range(NY):
                 for i in range(CAP):
                     row = jnp.broadcast_to(lr[o, i, pl.ds(zz, 1), :], (32, HID))
@@ -332,19 +343,21 @@
                     for b in range(NB):
                         value = jnp.where(row == b, blocks[b], value)
                     if o:
-                        bs[q, o, i, part, :] = value.astype(BF)
+                        bs[q, o, i, u, part, :] = value.astype(BF)
                     else:
-                        br[q, 0, i, part, :] = value.astype(BF)
+                        br[q, 0, i, u, part, :] = value.astype(BF)
             return inner
 
-        lax.fori_loop(0, BLK // 32, rows, 0)
+        lax.fori_loop(0, HALF // 32, rows, 0)
         for o in range(1, NY):
-            yb_copy(q, o).start()
+            yb_copy(q, o, u).start()
 
     def backward(q):
         zz = near_first(q)
         for o in range(1, NY):
-            pltpu.make_async_copy(br.at[q, o], br.at[q, o], yb_r.at[q, o]).wait()
+            for u in range(2):
+                piece = br.at[q, o, :, u]
+                pltpu.make_async_copy(piece, piece, yb_r.at[q, o, u]).wait()
 
         def pair(r, carry):
             at = ((y + r) % NY) * NZ + zz
@@ -428,38 +441,36 @@
             wg_out[pl.ds(r * 8, 8), pl.ds(HID * (1 - h) + q * 128, 128)] = yg[h, (n - d + ND) % ND]
 
     gacc[...] = jnp.zeros_like(gacc)
-    ag_first(0).start()
-    ag_first(1).start()
-    answer(0)
+    for u in range(2):
+        pointwise(u)
+        for way in range(2):
+            ag_copy(0, way, u).start()
+        answer(0, u)
+
+    def pass_on(k):
+        for u in range(2):
+            for way in range(2):
+                ag_copy(k - 1, way, u).wait_recv()
+                if k < NZ // 2:
+                    ag_copy(k, way, u).start()
+            if k < NZ // 2:
+                answer(2 * k - 1, u)
+                answer(2 * k, u)
+            else:
+                answer(NZ - 1, u)
+
     red_0(0, gs[...])
-    ag_first(0).wait_recv()
-    ag_first(1).wait_recv()
-    ag_next(1, 0).start()
-    ag_next(1, 1).start()
-    answer(1)
-    answer(2)
+    pass_on(1)
     red_1(0)
-    ag_next(1, 0).wait_recv()
-    ag_next(1, 1).wait_recv()
-    ag_next(2, 0).start()
-    ag_next(2, 1).start()
-    answer(3)
-    answer(4)
+    backward(0)
+    pass_on(2)
     red_2(0)
-    backward(0)
-    ag_next(2, 0).wait_recv()
-    ag_next(2, 1).wait_recv()
-    ag_last(0).start()
-    ag_last(1).start()
-    answer(5)
-    answer(6)
+    backward(1)
+    pass_on(3)
     red_3(0)
-    backward(1)
-    ag_last(0).wait_recv()
-    ag_last(1).wait_recv()
-    answer(7)
+    backward(2)
+    pass_on(4)
     red_4(0)
-    backward(2)
     backward(3)
     for q in range(4, NZ):
         backward(q)
@@ -482,14 +493,16 @@
     for t in range(NZ):
         for o in range(1, NY):
             yf_copy(t, o).wait_send()
-            yb_copy(t, o).wait_send()
-        if t < NZ - 1:
+            for u in range(2):
+                yb_copy(t, o, u).wait_send()
+        if 3 <= t < NZ - 1:
             zf_copy(t).wait_send()
     for way in range(2):
-        ag_first(way).wait_send()
-        ag_next(1, way).wait_send()
-        ag_next(2, way).wait_send()
-        ag_last(way).wait_send()
+        zx_copy(way).wait_send()
+        zy_copy(way).wait_send()
+        for k in range(NZ // 2):
+            for u in range(2):
+                ag_copy(k, way, u).wait_send()
     for h in range(2):
         for o in range(NX):
             rc_copy(h, o).wait_send()
@@ -521,10 +534,12 @@
         pltpu.VMEM((NZ, NY, CAP, BLK, HID), BF),
         pltpu.VMEM((NZ, NB, BLK, HID), BF),
         pltpu.VMEM((NZ, NB, BLK, HID), BF),
+        pltpu.VMEM((2, 2, BLK, HID), BF),
+        pltpu.VMEM((2, NB, BLK, HID), BF),
         pltpu.VMEM((ROWS, HID), F32),
-        pltpu.VMEM((NZ, NB, BLK, HID), BF),
-        pltpu.VMEM((NZ, NY, CAP, BLK, HID), BF),
-        pltpu.VMEM((NZ, NY, CAP, BLK, HID), BF),
+        pltpu.VMEM((NZ, NB, 2, HALF, HID), BF),
+        pltpu.VMEM((NZ, NY, CAP, 2, HALF, HID), BF),
+        pltpu.VMEM((NZ, NY, CAP, 2, HALF, HID), BF),
         pltpu.VMEM((ROWS, HID), BF),
         pltpu.VMEM((ROWS, HID), F32),
         pltpu.VMEM((2, NX, BLK, HID), F32),
@@ -538,8 +553,8 @@
         dma((5,)),
         dma((NF,)), dma((NF,)), dma((NX,)), dma((NX,)), dma((NX, NY)), dma((NX, NY)),
         dma((NX,)), dma((NX,)), dma((NY,)), dma((NY,)),
-        dma((NZ, NY)), dma((NZ, NY)), dma((NZ,)), dma((NZ,)), dma((NZ,)), dma((NZ,)),
-        dma((NZ, NY)), dma((NZ, NY)),
+        dma((NZ, NY)), dma((NZ, NY)), dma((NZ,)), dma((NZ,)), dma((2,)), dma((2,)), dma((2,)), dma((2,)),
+        dma((NZ, 2)), dma((NZ, 2)), dma((NZ, NY, 2)), dma((NZ, NY, 2)),
         dma((2, NX)), dma((2, NX)), dma((2, NX)), dma((2, NX)),
         dma((2,)), dma((2,)), dma((2,)), dma((2,)),
     ]

time: 170 us -> 161 us (0.947)
  Pallas kernels: 166 us -> 156 us
    pallas_call x1, Pallas kernels: 166 us -> 156 us  [local(): pl.pallas_call(main_kernel, out_shape=(jax.ShapeDtypeStruct((ROWS, HID),...]
where the time goes in v3:
time: 161 us; the launch traced here: 160 us
  Pallas kernels  156 us (97%)
  local copies, waits for them, and re-layouts  3.34 us (2%)
    pallas_call x1, Pallas kernels, local(): pl.pallas_call(main_kernel, out_shape=(jax.ShapeDtypeStruct((ROWS, HID),...  156 us
    unnamed x2, local copies, waits for them, and re-layouts  3.34 us

profile of v3, /device:TPU:1, one launch (start us, length us, event | category | flops | bytes accessed | tf_op | source)
XLA Modules:
  0.0 160.4 jit_solution(1217848304065406585)
XLA Ops:
  0.6 156.5 %shard_map.95 = (bf16[512,256]{1,0:T(8,128)(2,1)}, f32[128,512]{1,0:T(8,128)}) custom-call(s32[1,32]{1,0:T(1,128)} %bitcast.8, s32[1,32]{1,0:T(1,128)} %bitcast.9, s32[4,32]{1,0:T(4,128)} %bitcast.6, s32[4,128]{1,0:T(4,128)} %bitcast.7, bf16[8,512,128]{2,1,0:T(8,128)(2,1)} %bitcast.5, bf16[128,512]{1,0:T(8,128)(2,1)} %proj.1, ...), custom_call_target="tpu_custom_call" | custom-call | tf_op jit(solution)/shard_map/pallas_call | solution.py:561
  157.1 1.7 %copy.12 = bf16[512,256]{1,0:T(8,128)(2,1)} copy(bf16[512,256]{1,0:T(8,128)(2,1)} %get-tuple-element.4) | data formatting | bytes 524288
  158.8 1.7 %copy.13 = f32[128,512]{1,0:T(8,128)} copy(f32[128,512]{1,0:T(8,128)} %get-tuple-element.5) | data formatting | bytes 524288

commit v4 on v3

--- a/solution.py
+++ b/solution.py
@@ -11,6 +11,10 @@
 ND = NY * NZ
 FAR_FIRST = ((2, 0), (2, 1), (1, 0), (3, 0), (1, 1), (3, 1), (0, 1))
 NEAR_FIRST = FAR_FIRST[::-1]
+PLANE = sorted(
+    [(oy, oz) for oy in range(NY) for oz in range(NZ) if oy or oz],
+    key=lambda o: (-min(o[0], NY - o[0]) - min(o[1], NZ - o[1]), o),
+)
 BLK = 128
 HALF = 64
 NB = 4
@@ -59,9 +63,11 @@
     barrier = pltpu.get_barrier_semaphore()
     for o in range(1, NF):
         pl.semaphore_signal(barrier, inc=1, device_id=to_feat((f + o) % NF), device_id_type=MESH)
-    for o in range(1, ND):
-        pl.semaphore_signal(barrier, inc=1, device_id=((d + o) % ND, f), device_id_type=MESH)
-    pl.semaphore_wait(barrier, NF + ND - 2)
+    for o in range(1, NY):
+        pl.semaphore_signal(barrier, inc=1, device_id=to_yz((y + o) % NY, z), device_id_type=MESH)
+    for o in (1, 2, NZ - 2, NZ - 1):
+        pl.semaphore_signal(barrier, inc=1, device_id=to_yz(y, (z + o) % NZ), device_id_type=MESH)
+    pl.semaphore_wait(barrier, NF + NY + 2)
 
     def f_copy(ox, oc):
         g = ((x + ox) % NX) * NC + (c + oc) % NC
@@ -378,12 +384,12 @@
             x1.at[h, xx], rx.at[h, NX - o], rx_s.at[h, o], rx_r.at[h, NX - o], to_feat(xx * NC + c)
         )
 
-    def ry_copy(h, o):
-        e = (d + o) % ND
-        return remote(y1.at[h, e], ry.at[h, ND - o], ry_s.at[h], ry_r.at[h], (e, f))
-
-    def yg_copy(h, o):
-        return remote(yt.at[h], yg.at[h, ND - o], yg_s.at[h], yg_r.at[h], ((d + o) % ND, f))
+    def plane_copies(a, b, s, r, h, per_device):
+        for oy, oz in PLANE:
+            e = ((y + oy) % NY) * NZ + (z + oz) % NZ
+            back = ((NY - oy) % NY) * NZ + (NZ - oz) % NZ
+            part = a.at[h, e] if per_device else a.at[h]
+            remote(part, b.at[h, back], s.at[h], r.at[h], (e, f)).start()
 
     def red_0(h, grad):
         for o in (2, 1, 3, 0):
@@ -411,34 +417,27 @@
             r, q = n // 2, n % 2
             y1[h, n] = total[r * 8 : r * 8 + 8, q * 128 : q * 128 + 128]
 
-        def send(o, carry):
-            ry_copy(h, o).start()
-            return carry
-
-        lax.fori_loop(1, ND, send, 0)
+    def red_3(h):
+        plane_copies(y1, ry, ry_s, ry_r, h, True)
 
     def others(buf, h):
         return buf.at[h, pl.ds(1, ND - 1)]
 
-    def red_3(h):
+    def red_4(h):
         total = y1[h, d]
         pltpu.make_async_copy(others(ry, h), others(ry, h), ry_r.at[h]).wait()
         for o in range(1, ND):
             total = total + ry[h, o]
         yt[h] = total
         yg[h, 0] = total
-
-        def send(o, carry):
-            yg_copy(h, o).start()
-            return carry
-
-        lax.fori_loop(1, ND, send, 0)
-
-    def red_4(h):
+        plane_copies(yt, yg, yg_s, yg_r, h, False)
+
+    def red_5(h):
         pltpu.make_async_copy(others(yg, h), others(yg, h), yg_r.at[h]).wait()
         for n in range(ND):
             r, q = n // 2, n % 2
-            wg_out[pl.ds(r * 8, 8), pl.ds(HID * (1 - h) + q * 128, 128)] = yg[h, (n - d + ND) % ND]
+            back = ((n // NZ - y + NY) % NY) * NZ + (n % NZ - z + NZ) % NZ
+            wg_out[pl.ds(r * 8, 8), pl.ds(HID * (1 - h) + q * 128, 128)] = yg[h, back]
 
     gacc[...] = jnp.zeros_like(gacc)
     for u in range(2):
@@ -467,18 +466,22 @@
     red_2(0)
     backward(1)
     pass_on(3)
-    red_3(0)
     backward(2)
     pass_on(4)
-    red_4(0)
     backward(3)
     for q in range(4, NZ):
         backward(q)
 
     grad = gacc[...].astype(BF)
     red_0(1, grad)
-    for step in (red_1, red_2, red_3, red_4):
-        step(1)
+    red_1(1)
+    red_3(0)
+    red_2(1)
+    red_3(1)
+    red_4(0)
+    red_4(1)
+    red_5(0)
+    red_5(1)
 
     for ox, oc in FAR_FIRST:
         f_copy(ox, oc).wait_send()

time: 161 us -> 157 us (0.975)
  Pallas kernels: 156 us -> 152 us
    pallas_call x1, Pallas kernels: 156 us -> 152 us  [local(): pl.pallas_call(main_kernel, out_shape=(jax.ShapeDtypeStruct((ROWS, HID),...]
where the time goes in v4:
time: 157 us; the launch traced here: 156 us
  Pallas kernels  152 us (97%)
  local copies, waits for them, and re-layouts  3.34 us (2%)
    pallas_call x1, Pallas kernels, local(): pl.pallas_call(main_kernel, out_shape=(jax.ShapeDtypeStruct((ROWS, HID),...  152 us
    unnamed x2, local copies, waits for them, and re-layouts  3.34 us

profile of v4, /device:TPU:1, one launch (start us, length us, event | category | flops | bytes accessed | tf_op | source)
XLA Modules:
  0.0 156.5 jit_solution(10192418855887422011)
XLA Ops:
  0.6 152.5 %shard_map.95 = (bf16[512,256]{1,0:T(8,128)(2,1)}, f32[128,512]{1,0:T(8,128)}) custom-call(s32[1,32]{1,0:T(1,128)} %bitcast.8, s32[1,32]{1,0:T(1,128)} %bitcast.9, s32[4,32]{1,0:T(4,128)} %bitcast.6, s32[4,128]{1,0:T(4,128)} %bitcast.7, bf16[8,512,128]{2,1,0:T(8,128)(2,1)} %bitcast.5, bf16[128,512]{1,0:T(8,128)(2,1)} %proj.1, ...), custom_call_target="tpu_custom_call" | custom-call | tf_op jit(solution)/shard_map/pallas_call | solution.py:564
  153.1 1.7 %copy.12 = bf16[512,256]{1,0:T(8,128)(2,1)} copy(bf16[512,256]{1,0:T(8,128)(2,1)} %get-tuple-element.4) | data formatting | bytes 524288
  154.8 1.7 %copy.13 = f32[128,512]{1,0:T(8,128)} copy(f32[128,512]{1,0:T(8,128)} %get-tuple-element.5) | data formatting | bytes 524288

commit v5 on v4

--- a/solution.py
+++ b/solution.py
@@ -10,7 +10,7 @@
 NF = NX * NC
 ND = NY * NZ
 FAR_FIRST = ((2, 0), (2, 1), (1, 0), (3, 0), (1, 1), (3, 1), (0, 1))
-NEAR_FIRST = FAR_FIRST[::-1]
+ARRIVAL = ((0, 1), (1, 0), (3, 0), (1, 1), (3, 1), (2, 0), (2, 1))
 PLANE = sorted(
     [(oy, oz) for oy in range(NY) for oz in range(NZ) if oy or oz],
     key=lambda o: (-min(o[0], NY - o[0]) - min(o[1], NZ - o[1]), o),
@@ -32,7 +32,7 @@
     fb, pb, tb, ogb, nb, selfb, ftb, wt, tabv, tabs, inv_deg,
     ls, lr, cs, yr, ms, zr, zx, zy, sm,
     ga, bs, br, gs, gacc,
-    pw, rc, x1, rx, y1, ry, yt, yg,
+    pw, rc, x1, rx, xs, y1, ry, yt, yg,
     loc_sem, f_s, f_r, px_s, px_r, py_s, py_r, pc_s, pc_r, l_s, l_r,
     yf_s, yf_r, zf_s, zf_r, zx_s, zx_r, zy_s, zy_r, ag_s, ag_r, yb_s, yb_r,
     rc_s, rc_r, rx_s, rx_r, ry_s, ry_r, yg_s, yg_r,
@@ -160,13 +160,13 @@
     table.wait()
 
     own_f.wait()
-    for o in range(NX):
-        shard = pb.at[(x + o) % NX, 1 - c]
-        pltpu.make_async_copy(shard, shard, pc_r.at[o]).wait()
     sm[...] = jnp.dot(fb[f], pb[x, c, :, :HID], preferred_element_type=F32)
-    for ox, oc in NEAR_FIRST:
+    for ox, oc in ARRIVAL:
         xx, cc = (x + ox) % NX, (c + oc) % NC
         g = xx * NC + cc
+        if oc:
+            shard = pb.at[xx, cc]
+            pltpu.make_async_copy(shard, shard, pc_r.at[ox]).wait()
         pltpu.make_async_copy(fb.at[g], fb.at[g], f_r.at[ox * NC + oc]).wait()
         sm[...] += jnp.dot(fb[g], pb[xx, cc, :, :HID], preferred_element_type=F32)
     nb[...] = sm[...].astype(BF).reshape(NB, BLK, HID)
@@ -215,7 +215,7 @@
     lax.fori_loop(0, NZ, contribute, 0)
 
     sm[...] = jnp.dot(fb[f], pb[x, c, :, HID:], preferred_element_type=F32)
-    for ox, oc in NEAR_FIRST:
+    for ox, oc in ARRIVAL:
         xx, cc = (x + ox) % NX, (c + oc) % NC
         sm[...] += jnp.dot(fb[xx * NC + cc], pb[xx, cc, :, HID:], preferred_element_type=F32)
     selfb[...] = sm[...].astype(BF)
@@ -288,7 +288,7 @@
             lax.fori_loop(0, most if t < NZ - 2 else SLOTS - t * most, turn, 0)
             for g in (t, NZ - 1) if t == NZ - 2 else (t,):
                 for b in range(NB):
-                    ftb[g, :, pl.ds(b * BLK, BLK)] = fb[g, pl.ds(b * BLK, BLK), :].T
+                    ftb[g % NC, g // NC, :, pl.ds(b * BLK, BLK)] = fb[g, pl.ds(b * BLK, BLK), :].T
 
     for t in range(NZ):
         merge(t)
@@ -381,7 +381,7 @@
     def rx_copy(h, o):
         xx = (x + o) % NX
         return remote(
-            x1.at[h, xx], rx.at[h, NX - o], rx_s.at[h, o], rx_r.at[h, NX - o], to_feat(xx * NC + c)
+            xs.at[h, xx], rx.at[h, NX - o], rx_s.at[h, o], rx_r.at[h, NX - o], to_feat(xx * NC + c)
         )
 
     def plane_copies(a, b, s, r, h, per_device):
@@ -392,13 +392,14 @@
             remote(part, b.at[h, back], s.at[h], r.at[h], (e, f)).start()
 
     def red_0(h, grad):
+        def term(parity):
+            left = ftb[parity].reshape(NX * BLK, ROWS)
+            return jnp.dot(left, grad, preferred_element_type=F32).reshape(NX, BLK, HID)
+
+        pw[h] = term(1 - c)
         for o in (2, 1, 3, 0):
-            xx = (x + o) % NX
-            pw[h, xx] = jnp.dot(ftb[xx * NC + 1 - c], grad, preferred_element_type=F32)
             rc_copy(h, o).start()
-        for o in (2, 1, 3, 0):
-            xx = (x + o) % NX
-            x1[h, xx] = jnp.dot(ftb[xx * NC + c], grad, preferred_element_type=F32)
+        x1[h] = term(c)
 
     def red_1(h):
         for o in (2, 1, 3, 0):
@@ -406,13 +407,14 @@
             rc_copy(h, o).wait_recv()
             x1[h, xx] = x1[h, xx] + rc[h, xx]
             if o:
+                xs[h, xx] = x1[h, xx].astype(BF)
                 rx_copy(h, o).start()
 
     def red_2(h):
         total = x1[h, x]
         for o in (1, 3, 2):
             pltpu.make_async_copy(rx.at[h, o], rx.at[h, o], rx_r.at[h, o]).wait()
-            total = total + rx[h, o]
+            total = total + rx[h, o].astype(F32)
         for n in range(ND):
             r, q = n // 2, n % 2
             y1[h, n] = total[r * 8 : r * 8 + 8, q * 128 : q * 128 + 128]
@@ -526,7 +528,7 @@
         pltpu.VMEM((ROWS, HID), BF),
         pltpu.VMEM((NB, BLK, HID), BF),
         pltpu.VMEM((ROWS, HID), BF),
-        pltpu.VMEM((NF, BLK, ROWS), BF),
+        pltpu.VMEM((NC, NX, BLK, ROWS), BF),
         pltpu.VMEM((SLOTS, NB * BLK, BLK), BF),
         pltpu.VMEM((CAP + 1, ND, 128), jnp.int32),
         pltpu.SMEM((CAP + 1, ND, 128), jnp.int32),
@@ -548,7 +550,8 @@
         pltpu.VMEM((2, NX, BLK, HID), F32),
         pltpu.VMEM((2, NX, BLK, HID), F32),
         pltpu.VMEM((2, NX, BLK, HID), F32),
-        pltpu.VMEM((2, NX, BLK, HID), F32),
+        pltpu.VMEM((2, NX, BLK, HID), BF),
+        pltpu.VMEM((2, NX, BLK, HID), BF),
         pltpu.VMEM((2, ND, 8, 128), F32),
         pltpu.VMEM((2, ND, 8, 128), F32),
         pltpu.VMEM((2, 8, 128), F32),

time: 157 us -> 153 us (0.975)
  Pallas kernels: 152 us -> 149 us
    pallas_call x1, Pallas kernels: 152 us -> 149 us  [local(): pl.pallas_call(main_kernel, out_shape=(jax.ShapeDtypeStruct((ROWS, HID),...]
where the time goes in v5:
time: 153 us
  Pallas kernels  149 us (97%)
  local copies, waits for them, and re-layouts  3.34 us (2%)
    pallas_call x1, Pallas kernels, local(): pl.pallas_call(main_kernel, out_shape=(jax.ShapeDtypeStruct((ROWS, HID),...  149 us
    unnamed x2, local copies, waits for them, and re-layouts  3.34 us

profile of v5, /device:TPU:1, one launch (start us, length us, event | category | flops | bytes accessed | tf_op | source)
XLA Modules:
  0.0 152.5 jit_solution(17063687020667438283)
XLA Ops:
  0.6 148.5 %shard_map.95 = (bf16[512,256]{1,0:T(8,128)(2,1)}, f32[128,512]{1,0:T(8,128)}) custom-call(s32[1,32]{1,0:T(1,128)} %bitcast.8, s32[1,32]{1,0:T(1,128)} %bitcast.9, s32[4,32]{1,0:T(4,128)} %bitcast.6, s32[4,128]{1,0:T(4,128)} %bitcast.7, bf16[8,512,128]{2,1,0:T(8,128)(2,1)} %bitcast.5, bf16[128,512]{1,0:T(8,128)(2,1)} %proj.1, ...), custom_call_target="tpu_custom_call" | custom-call | tf_op jit(solution)/shard_map/pallas_call | solution.py:567
  149.2 1.7 %copy.12 = bf16[512,256]{1,0:T(8,128)(2,1)} copy(bf16[512,256]{1,0:T(8,128)(2,1)} %get-tuple-element.4) | data formatting | bytes 524288
  150.8 1.7 %copy.13 = f32[128,512]{1,0:T(8,128)} copy(f32[128,512]{1,0:T(8,128)} %get-tuple-element.5) | data formatting | bytes 524288

commit v6 on v5

--- a/solution.py
+++ b/solution.py
@@ -191,8 +191,7 @@
 
     def contribute(t, carry):
         zz = far_first(t)
-        for o in range(1, NY + 1):
-            r = o % NY
+        for r in (2, 1, 3, 0):
             yy = (y + r) % NY
             for i in range(CAP):
                 s = slot_at(i, yy * NZ + zz)
@@ -355,7 +354,7 @@
             return inner
 
         lax.fori_loop(0, HALF // 32, rows, 0)
-        for o in range(1, NY):
+        for o in (2, 1, 3):
             yb_copy(q, o, u).start()
 
     def backward(q):
@@ -574,17 +573,22 @@
         out_specs=[vmem] * 2,
         scratch_shapes=scratch,
         compiler_params=pltpu.CompilerParams(
-            collective_id=0, has_side_effects=True, vmem_limit_bytes=60 << 20
+            collective_id=0, has_side_effects=True, vmem_limit_bytes=53 << 20
         ),
     )(
-        slot_owner.reshape(1, SLOTS),
-        slot_block.reshape(1, SLOTS),
-        source_block.T,
-        counts.reshape(NB, BLK),
-        feats.reshape(NF, ROWS, BLK),
-        projection,
-        tiles,
-        out_grad,
+        *(
+            pltpu.with_memory_space_constraint(array, pltpu.HBM)
+            for array in (
+                slot_owner.reshape(1, SLOTS),
+                slot_block.reshape(1, SLOTS),
+                source_block.T,
+                counts.reshape(NB, BLK),
+                feats.reshape(NF, ROWS, BLK),
+                projection,
+                tiles,
+                out_grad,
+            )
+        )
     )
 
 

time: 153 us -> 149 us (0.974)
  Pallas kernels: 149 us -> 147 us
  local copies, waits for them, and re-layouts: 3.34 us -> 1.41 us
    unnamed x2, local copies, waits for them, and re-layouts: 3.34 us -> 1.41 us
    pallas_call x1, Pallas kernels: 149 us -> 147 us  [local(): pl.pallas_call(main_kernel, out_shape=(jax.ShapeDtypeStruct((ROWS, HID),...]
where the time goes in v6:
time: 149 us
  Pallas kernels  147 us (99%)
    pallas_call x1, Pallas kernels, local(): pl.pallas_call(main_kernel, out_shape=(jax.ShapeDtypeStruct((ROWS, HID),...  147 us

profile of v6, /device:TPU:1, one launch (start us, length us, event | category | flops | bytes accessed | tf_op | source)
XLA Modules:
  0.0 148.7 jit_solution(14418401096214218056)
XLA Ops:
  0.6 146.6 %shard_map.95 = (bf16[512,256]{1,0:T(8,128)(2,1)S(1)}, f32[128,512]{1,0:T(8,128)S(1)}) custom-call(s32[1,32]{1,0:T(1,128)} %bitcast.8, s32[1,32]{1,0:T(1,128)} %bitcast.9, s32[4,32]{1,0:T(4,128)} %bitcast.6, s32[4,128]{1,0:T(4,128)} %bitcast.7, bf16[8,512,128]{2,1,0:T(8,128)(2,1)} %bitcast.5, bf16[128,512]{1,0:T(8,128)(2,1)} %proj.1, ...), custom_call_target="tpu_custom_call" | custom-call | tf_op jit(solution)/shard_map/pallas_call | solution.py:566
  147.2 0.7 copy.12
  148.0 0.7 copy.13
